TPU v7x, 256 devices: a whole 4x4x8 slice. The times are simulated.
256 devices in a mesh: comp: 2 (over y_hi), lat: 8 (over x, core), lon: 16 (over y_lo, z).
Axes of the slice: x: 4, y: 4 (y_hi: 2, y_lo: 2; y = y_hi * 2 + y_lo), z: 8, core: 2. Of those that a mesh axis runs over, the one named last changes fastest.
Arguments:
- atm_state: bfloat16 [32768, 512], P(('comp', 'lat', 'lon')), may hold values from -6 to 6
- edge_state: bfloat16 [32768, 6, 512], P(('comp', 'lat', 'lon')), may hold values from -6 to 6
- neighbours: int32 [32768, 6], P(('comp', 'lat', 'lon')), may hold values from 0 to 32767, as said below
- degree: int32 [32768], P(('comp', 'lat', 'lon')), may hold values from 5 to 6
- surface_fields: float32 [4, 512, 2048], P(None, ('comp', 'lat'), 'lon'), may hold values from -6 to 6
- ocean_state: bfloat16 [512, 2048, 256], P(('comp', 'lat'), 'lon'), may hold values from -6 to 6
- wet_mask: int32 [512, 2048], P(('comp', 'lat'), 'lon'), may hold values from 0 to 1, as said below
- flux_columns: int32 [4, 512, 2048], P(None, ('comp', 'lat'), 'lon'), may hold values from 0 to 32767, as said below
- flux_weights: float32 [4, 512, 2048], P(None, ('comp', 'lat'), 'lon'), may hold values from 0.1 to 1
- surface_columns: int32 [4, 32768], P(None, ('comp', 'lat', 'lon')), may hold values from 0 to 1048575, as said below
- surface_weights: float32 [4, 32768], P(None, ('comp', 'lat', 'lon')), may hold values from 0.1 to 1
- w_surface: float32 [4, 512], replicated, may hold values from -3 to 3
- w_flux: float32 [512, 4], replicated, may hold values from -0.25 to 0.25
- ln1_gain: float32 [512], replicated, may hold values from 0.5 to 1.5
- w_query: bfloat16 [512, 512], replicated, may hold values from -0.25 to 0.25
- w_key: bfloat16 [512, 512], replicated, may hold values from -0.25 to 0.25
- w_value: bfloat16 [512, 512], replicated, may hold values from -0.25 to 0.25
- w_out: bfloat16 [512, 512], replicated, may hold values from -0.25 to 0.25
- w_edge_in: bfloat16 [512, 512], replicated, may hold values from -0.25 to 0.25
- w_edge_src: bfloat16 [512, 512], replicated, may hold values from -0.25 to 0.25
- w_edge_dst: bfloat16 [512, 512], replicated, may hold values from -0.25 to 0.25
- w_edge_out: bfloat16 [512, 512], replicated, may hold values from -0.25 to 0.25
- w_bias: float32 [512, 8], replicated, may hold values from -0.25 to 0.25
- ln2_gain: float32 [512], replicated, may hold values from 0.5 to 1.5
- w_up: bfloat16 [512, 2048], replicated, may hold values from -0.25 to 0.25
- w_down: bfloat16 [2048, 512], replicated, may hold values from -0.125 to 0.125
- w_flux_in: float32 [4, 256], replicated, may hold values from -3 to 3
- dw_kernel: float32 [2, 49, 256], replicated, may hold values from -0.875 to 0.875
- dw_bias: float32 [2, 256], replicated, may hold values from -3 to 3
- ocean_gain: float32 [2, 256], replicated, may hold values from 0.5 to 1.5
- w_expand: bfloat16 [2, 256, 1024], replicated, may hold values from -0.375 to 0.375
- w_reduce: bfloat16 [2, 1024, 256], replicated, may hold values from -0.1875 to 0.1875
- layer_scale: float32 [2, 256], replicated, may hold values from 0.2 to 1
Outputs:
- atm_out: bfloat16 [32768, 512], P(('comp', 'lat', 'lon'))
- edge_out: bfloat16 [32768, 6, 512], P(('comp', 'lat', 'lon'))
- ocean_out: bfloat16 [512, 2048, 256], P(('comp', 'lat'), 'lon')
Inputs may be any that keep to these rules, and one draw needn't show every extreme that they name: `neighbours`: slots beyond degree[n] hold n itself. A used slot names a node of the same partition, or one of the first 64 nodes of one of the eight partitions beside it (partitions are numbered row by row over 16 rows of 16, each holding 128 consecutive ids; columns wrap around, rows do not). `wet_mask`: the first and last 3 latitude rows are land. `flux_columns`: each ocean cell reads nodes of the partitions of its own row band (latitude row // 32), in any column. `surface_columns`: each node reads cells whose latitude row // 32 is its partition's row, in any longitude.
All inputs are finite; a program needn't handle non-finite values.
Results may differ from a plain program's by a relative error of at most 0.011.
Values may be sent and summed in bfloat16 or wider, within the bound.
A program may use at most 128 MiB of HBM per device.

v0:
```python
import functools
import jax
import jax.numpy as jnp
from jax import lax
from jax.experimental import pallas as pl
from jax.experimental.pallas import tpu as pltpu
from jax.sharding import PartitionSpec as P

F32 = jnp.float32
BF16 = jnp.bfloat16


def iota(shape, axis):
    return lax.broadcasted_iota(jnp.int32, shape, axis)


def swap_blocks(parts):
    lane = iota(parts[0].shape, 1)
    upper = lane >= 64
    odd = (lane // 32) % 2 == 1
    first = []
    for low in range(2):
        a, b = parts[low], parts[low + 2]
        first.append((jnp.where(upper, pltpu.roll(b, 64, 1), a), jnp.where(upper, b, pltpu.roll(a, 64, 1))))
    out = [None] * 4
    for side in range(2):
        a, b = first[0][side], first[1][side]
        out[2 * side] = jnp.where(odd, pltpu.roll(b, 32, 1), a)
        out[2 * side + 1] = jnp.where(odd, b, pltpu.roll(a, 96, 1))
    return out


def order_matrix():
    row, col = iota((128, 128), 0), iota((128, 128), 1)
    return jnp.where(col == 8 * (row % 16) + row // 16, 1.0, 0.0)


def build_weights(block, kernel_ref, w_ref):
    eye = (iota((32, 256), 0) == iota((32, 256), 1) % 32)

    def body(tap, carry):
        rows = kernel_ref[pl.ds(tap * 7, 7), block]
        stack = jnp.concatenate([rows, jnp.zeros((17, 256), F32)], axis=0)
        shifted = [stack if j == 0 else pltpu.roll(stack, j, 0) for j in range(8)]
        for t in range(2):
            halves = []
            for h in range(2):
                halves.append(swap_blocks([shifted[4 * h + i][0:16, 128 * t : 128 * t + 128] for i in range(4)]))
            for u in range(4):
                line = jnp.concatenate([halves[0][u], halves[1][u]], axis=1)
                for n in range(16):
                    piece = jnp.where(eye, jnp.broadcast_to(line[n : n + 1], (32, 256)), 0.0)
                    w_ref[4 * t + u, pl.ds(tap * 512 + n * 32, 32)] = piece.astype(BF16)
        return carry

    lax.fori_loop(0, 7, body, 0)


def fill_rows(tile_of, west, east, xt_ref, row):
    first = iota((16, 256), 0) == 0
    last = iota((16, 256), 0) == 15
    plain = [tile_of(j) for j in range(8)]
    zero_view, one_view = [None] * 8, [None] * 8
    for p in range(8):
        if p < 3:
            data = plain[p + 5]
            one_view[p] = data
            edge = jnp.broadcast_to(west[p + 4 : p + 5], (16, 256))
            zero_view[p] = jnp.where(first, edge, pltpu.roll(data.astype(F32), 1, 0)).astype(BF16)
        else:
            data = plain[p - 3]
            zero_view[p] = data
            rolled = pltpu.roll(data.astype(F32), 15, 0)
            if p < 6:
                rolled = jnp.where(last, jnp.broadcast_to(east[p - 3 : p - 2], (16, 256)), rolled)
            one_view[p] = rolled.astype(BF16)
    for q, view in enumerate((zero_view, one_view)):
        for t in range(2):
            for h in range(2):
                done = swap_blocks([view[4 * h + i][:, 128 * t : 128 * t + 128] for i in range(4)])
                for u in range(4):
                    xt_ref[q, 4 * t + u, row, :, 128 * h : 128 * h + 128] = done[u]


def block_body(last, kernel_ref, bias_ref, gain_ref, scale_ref, up_ref, down_ref, mask_ref, x_ref, north_ref, south_ref,
               west_ref, east_ref, nw_ref, ne_ref, sw_ref, se_ref, out_ref, edge_ref, w_ref, xt_ref, conv_ref, stat_ref, rms_ref):
    block = 1 if last else 0
    build_weights(block, kernel_ref, w_ref)

    def interior(r, carry):
        at = pl.multiple_of(r * 8, 8)
        fill_rows(lambda j: x_ref[r, j], west_ref[pl.ds(at, 8)].astype(F32), east_ref[pl.ds(at, 8)].astype(F32), xt_ref, r + 3)
        return carry

    lax.fori_loop(0, 32, interior, 0, unroll=2)
    for k in range(3):
        fill_rows(lambda j: north_ref[k, j], nw_ref[8 + 8 * k : 16 + 8 * k].astype(F32), ne_ref[8 + 8 * k : 16 + 8 * k].astype(F32), xt_ref, k)
        fill_rows(lambda j: south_ref[k, j], sw_ref[8 * k : 8 * k + 8].astype(F32), se_ref[8 * k : 8 * k + 8].astype(F32), xt_ref, 35 + k)

    grouped = []
    lines = jnp.concatenate([bias_ref[block : block + 1]] + [gain_ref[block : block + 1]] * 7, axis=0)
    scale = scale_ref[block : block + 1]
    for t in range(2):
        part = lines[:, 128 * t : 128 * t + 128]
        grouped += [jnp.concatenate([v, v], axis=1) for v in swap_blocks([part] * 4)]

    for g in range(8):
        pieces = []
        for a in range(7):
            for q in range(2):
                pieces.append(xt_ref[q, g, a : a + 32].reshape(512, 256))
        acc = jnp.dot(jnp.concatenate(pieces, axis=1), w_ref[g], preferred_element_type=F32) + grouped[g][0:1]
        conv_ref[g] = acc
        stat_ref[...] = acc if g == 0 else stat_ref[...] + acc

    same = jnp.where(iota((256, 256), 0) // 32 == iota((256, 256), 1) // 32, 1.0 / 256, 0.0).astype(BF16)
    same2 = jnp.concatenate([same, same], axis=0)

    def spread(values):
        high = values.astype(BF16)
        low = (values - high.astype(F32)).astype(BF16)
        return jnp.dot(jnp.concatenate([high, low], axis=1), same2, preferred_element_type=F32)

    stat_ref[...] = spread(stat_ref[...])

    def squares(n, carry):
        at = pl.ds(pl.multiple_of(n * 64, 64), 64)
        mean = stat_ref[at]
        total = None
        for g in range(8):
            centre = conv_ref[g, at] - mean
            total = centre * centre if total is None else total + centre * centre
        rms_ref[at] = total
        return carry

    lax.fori_loop(0, 8, squares, 0)
    rms_ref[...] = lax.rsqrt(spread(rms_ref[...]) + 1e-6)
    order = order_matrix()
    ones = jnp.ones((128, 256), BF16)
    order_back = jnp.where(iota((128, 128), 0) == 8 * (iota((128, 128), 1) % 16) + iota((128, 128), 1) // 16, 1.0, 0.0).astype(BF16)

    def mlp(n, carry):
        at = pl.ds(pl.multiple_of(n * 64, 64), 64)
        mean, rms = stat_ref[at], rms_ref[at]
        norm = [((conv_ref[g, at] - mean) * rms * grouped[g][1:2]).astype(BF16) for g in range(8)]
        tiles = [[None] * 2 for _ in range(8)]
        for h in range(2):
            for t in range(2):
                done = swap_blocks([norm[4 * t + u][:, 128 * h : 128 * h + 128] for u in range(4)])
                for i in range(4):
                    tiles[4 * h + i][t] = done[i]
        full = [jnp.concatenate(pair, axis=1) for pair in tiles]
        rows = jnp.concatenate([full[j][16 * k : 16 * k + 16] for k in range(4) for j in range(8)], axis=0)
        wide = jnp.dot(rows, up_ref[block], preferred_element_type=F32)
        grown = jax.nn.gelu(wide).astype(BF16)
        small = jnp.dot(grown, down_ref[block], preferred_element_type=F32)
        picks = jnp.concatenate([order * mask_ref[pl.ds(4 * n + k, 1)].astype(F32) for k in range(4)], axis=0).astype(BF16)
        sea = jnp.dot(picks, ones, preferred_element_type=F32)
        base = x_ref[pl.ds(4 * n, 4)].reshape(512, 256).astype(F32)
        fresh = sea * (base + scale * small)
        fresh16 = fresh.astype(BF16)
        if last:
            for k in range(4):
                natural = jnp.dot(order_back, fresh16[128 * k : 128 * k + 128], preferred_element_type=F32)
                out_ref[4 * n + k] = natural.astype(BF16)
        else:
            out_ref[pl.ds(4 * n, 4)] = fresh16.reshape(4, 8, 16, 256)
            lines = []
            for k in range(4):
                lines += edge_lines(fresh[128 * k : 128 * k + 128])
            edge_ref[pl.ds(pl.multiple_of(32 * n, 32), 32)] = jnp.concatenate(lines, axis=0).astype(BF16)
        return carry

    lax.fori_loop(0, 8, mlp, 0, unroll=2)


def edge_lines(rows):
    at = (0, 16, 32, 48, 95, 111, 127, 111)
    return [rows[p : p + 1] for p in at]


def ocean_block(last, kernel, bias, gain, scale, up, down, mask, x, halo):
    def body(*refs):
        ins, rest = refs[:16], refs[16:]
        if last:
            out_ref, scratch = rest[0], rest[1:]
            block_body(True, *ins, out_ref, None, *scratch)
        else:
            block_body(False, *ins, rest[0], rest[1], *rest[2:])

    vm = pl.BlockSpec(memory_space=pltpu.VMEM)
    args = (kernel.transpose(1, 0, 2), bias, gain, scale, up, down, mask, x) + tuple(halo)
    specs_in = [vm] * len(args)
    if last:
        shapes = jax.ShapeDtypeStruct((32, 128, 256), BF16)
        specs = vm
    else:
        shapes = (jax.ShapeDtypeStruct((32, 8, 16, 256), BF16), jax.ShapeDtypeStruct((256, 256), BF16))
        specs = (vm, vm)
    return pl.pallas_call(
        body,
        out_shape=shapes,
        in_specs=specs_in,
        out_specs=specs,
        scratch_shapes=[
            pltpu.VMEM((8, 3584, 256), BF16),
            pltpu.VMEM((2, 8, 38, 16, 256), BF16),
            pltpu.VMEM((8, 512, 256), F32),
            pltpu.VMEM((512, 256), F32),
            pltpu.VMEM((512, 256), F32),
        ],
        compiler_params=pltpu.CompilerParams(vmem_limit_bytes=60 << 20),
        name="ocean_last" if last else "ocean_first",
    )(*args)


def vmem():
    return pl.BlockSpec(memory_space=pltpu.VMEM)


def anywhere():
    return pl.BlockSpec(memory_space=pl.ANY)


def split(values):
    high = values.astype(BF16)
    return high, (values - high.astype(F32)).astype(BF16)


def contract_last(a, b):
    return lax.dot_general(a, b, (((1,), (1,)), ((), ())), preferred_element_type=F32)


def contract_first(a, b):
    return lax.dot_general(a, b, (((0,), (0,)), ((), ())), preferred_element_type=F32)


def unit_norm(values, gain, epsilon):
    centre = values - jnp.mean(values, axis=-1, keepdims=True)
    spread = jnp.mean(centre * centre, axis=-1, keepdims=True)
    return centre * lax.rsqrt(spread + epsilon) * gain


def gather_kernel(state_ref, wflux_ref, fields_ref, table_ref, own_ref, send_sem, recv_sem, local_sem):
    me = lax.axis_index("lon")
    high, low = split(wflux_ref[...])
    both = contract_last(jnp.concatenate([high, low], axis=0), state_ref[...])
    fluxes = both[0:4] + both[4:8]
    own_ref[0:128] = fields_ref[...].astype(BF16)
    own_ref[128:144] = jnp.concatenate([fluxes, jnp.zeros((12, 128), F32)], axis=0).astype(BF16)
    barrier = pltpu.get_barrier_semaphore()
    for step in range(1, 16):
        pl.semaphore_signal(barrier, inc=1, device_id={"lon": lax.rem(me + step, 16)}, device_id_type=pl.DeviceIdType.MESH)
    pl.semaphore_wait(barrier, 15)
    copies = []
    for step in range(1, 16):
        copy = pltpu.make_async_remote_copy(
            src_ref=own_ref, dst_ref=table_ref.at[me], send_sem=send_sem.at[step], recv_sem=recv_sem.at[step],
            device_id={"lon": lax.rem(me + step, 16)}, device_id_type=pl.DeviceIdType.MESH)
        copy.start()
        copies.append(copy)
    mine = pltpu.make_async_copy(own_ref, table_ref.at[me], local_sem)
    mine.start()
    mine.wait()
    for copy in copies:
        copy.wait()


def band_gather(state, wflux, fields):
    return pl.pallas_call(
        gather_kernel,
        out_shape=jax.ShapeDtypeStruct((16, 144, 128), BF16),
        in_specs=[vmem()] * 3,
        out_specs=anywhere(),
        scratch_shapes=[pltpu.VMEM((144, 128), BF16), pltpu.SemaphoreType.DMA((16,)), pltpu.SemaphoreType.DMA((16,)), pltpu.SemaphoreType.DMA],
        compiler_params=pltpu.CompilerParams(collective_id=0, has_side_effects=True),
        name="band_gather",
    )(state, wflux, fields)


def halo_kernel(with_rims, *refs):
    if with_rims:
        x_ref, edge_ref, norm_ref = refs[:3]
        rims_ref = refs[11]
        halo, send_sem, recv_sem = refs[3:11], refs[12], refs[13]
    else:
        x_ref, edge_ref = refs[:2]
        halo, send_sem, recv_sem = refs[2:10], refs[10], refs[11]
    north, south, west, east, nw, ne, sw, se = halo
    band = lax.axis_index("comp") * 8 + lax.axis_index("lat")
    col = lax.axis_index("lon")

    def device(dr, dc):
        row = lax.rem(band + 16 + dr, 16)
        return {"comp": row // 8, "lat": lax.rem(row, 8), "lon": lax.rem(col + 16 + dc, 16)}

    around = [(dr, dc) for dr in (-1, 0, 1) for dc in (-1, 0, 1) if (dr, dc) != (0, 0)]
    barrier = pltpu.get_barrier_semaphore()
    for dr, dc in around:
        pl.semaphore_signal(barrier, inc=1, device_id=device(dr, dc), device_id_type=pl.DeviceIdType.MESH)
    pl.semaphore_wait(barrier, 8)
    top, bottom = edge_ref.at[pl.ds(0, 32)], edge_ref.at[pl.ds(224, 32)]
    moves = [
        (x_ref.at[pl.ds(0, 3)], south, -1, 0),
        (x_ref.at[pl.ds(29, 3)], north, 1, 0),
        (edge_ref, east, 0, -1),
        (edge_ref, west, 0, 1),
        (top, se, -1, -1),
        (top, sw, -1, 1),
        (bottom, ne, 1, -1),
        (bottom, nw, 1, 1),
    ]
    if with_rims:
        for dr, dc in around:
            slot = (1 - dr) * 3 + 1 - dc
            slot = slot - 1 if slot > 4 else slot
            moves.append((norm_ref.at[pl.ds(0, 64)], rims_ref.at[slot], dr, dc))
    copies = []
    for n, (source, target, dr, dc) in enumerate(moves):
        copy = pltpu.make_async_remote_copy(
            src_ref=source, dst_ref=target, send_sem=send_sem.at[n], recv_sem=recv_sem.at[n],
            device_id=device(dr, dc), device_id_type=pl.DeviceIdType.MESH)
        copy.start()
        copies.append(copy)
    for copy in copies:
        copy.wait()


def exchange(x, edge, normed=None):
    rims = normed is not None
    shapes = [jax.ShapeDtypeStruct((3, 8, 16, 256), BF16)] * 2 + [jax.ShapeDtypeStruct((256, 256), BF16)] * 2
    shapes += [jax.ShapeDtypeStruct((32, 256), BF16)] * 4
    args = [x, edge]
    if rims:
        shapes.append(jax.ShapeDtypeStruct((8, 64, 512), BF16))
        args.append(normed)
    count = 16 if rims else 8
    return pl.pallas_call(
        functools.partial(halo_kernel, rims),
        out_shape=tuple(shapes),
        in_specs=[anywhere()] * len(args),
        out_specs=tuple([anywhere()] * len(shapes)),
        scratch_shapes=[pltpu.SemaphoreType.DMA((count,)), pltpu.SemaphoreType.DMA((count,))],
        compiler_params=pltpu.CompilerParams(collective_id=1 if rims else 2, has_side_effects=True),
        name="exchange_first" if rims else "exchange_second",
    )(*args)


def front_kernel(table_ref, cols_ref, fluxw_ref, ocean_ref, mask_ref, wfin_ref, scols_ref, sw_ref, state_ref, wsurf_ref, gain_ref,
                 x_ref, edge_ref, atm_ref, norm_ref):
    pairs = []
    for p in range(8):
        pairs.append(jnp.concatenate([table_ref[2 * p, 128:132], table_ref[2 * p + 1, 128:132]], axis=0))
    small = jnp.concatenate(pairs, axis=0)
    node = iota((128, 128), 0)
    half = iota((8, 128), 0) // 4
    wide = jnp.concatenate([wfin_ref[...], wfin_ref[...]], axis=0)
    whigh, wlow = split(wide)
    zero8 = jnp.zeros((8, 256), BF16)
    right = jnp.concatenate([
        jnp.concatenate([whigh, zero8], axis=1), jnp.concatenate([whigh, zero8], axis=1),
        jnp.concatenate([wlow, zero8], axis=1), jnp.concatenate([zero8, jnp.ones((8, 256), BF16)], axis=1)], axis=0)
    order = order_matrix().astype(BF16)
    top_row = iota((8, 128), 0) == 0

    def row(r, carry):
        ids = [cols_ref[k, pl.ds(r, 1)] for k in range(4)]
        hots = [jnp.where(node == (i & 127), 1.0, 0.0).astype(BF16) for i in ids]
        picked = jnp.dot(small, jnp.concatenate(hots, axis=1), preferred_element_type=F32)
        cell = None
        for k in range(4):
            part = (ids[k] >> 7) & 15
            level = part >> 1
            total = None
            for p in range(8):
                term = jnp.where(level == p, picked[8 * p : 8 * p + 8, 128 * k : 128 * k + 128], 0.0)
                total = term if total is None else total + term
            total = jnp.where(half == (part & 1), total, 0.0) * fluxw_ref[k, pl.ds(r, 1)]
            cell = total if cell is None else cell + total
        high, low = split(cell)
        sea = jnp.where(top_row, mask_ref[pl.ds(r, 1)].astype(F32), 0.0).astype(BF16)
        both = contract_first(jnp.concatenate([high, low, high, sea], axis=0), right)
        fresh = both[:, 256:512] * (ocean_ref[r].astype(F32) + both[:, 0:256])
        fresh16 = fresh.astype(BF16)
        x_ref[r] = jnp.dot(order, fresh16, preferred_element_type=F32).astype(BF16).reshape(8, 16, 256)
        line = jnp.concatenate([fresh[0:4], fresh[125:128], fresh[127:128]], axis=0)
        edge_ref[pl.ds(pl.multiple_of(r * 8, 8), 8)] = line.astype(BF16)
        return carry

    lax.fori_loop(0, 32, row, 0)

    ids = jnp.concatenate([scols_ref[k : k + 1] for k in range(4)], axis=1)
    cell = ids & 2047
    level = (ids >> 11) & 31
    spot = iota((128, 512), 0)
    hots, tabs = [], []
    for p in range(16):
        hots.append(jnp.where(spot + 128 * p == cell, 1.0, 0.0).astype(BF16))
        tabs.append(table_ref[p, 0:128])
    picked = jnp.dot(jnp.concatenate(tabs, axis=1), jnp.concatenate(hots, axis=0), preferred_element_type=F32)
    weight = jnp.concatenate([sw_ref[k : k + 1] for k in range(4)], axis=1)
    chosen = jnp.where(iota((32, 512), 0) == level, weight, 0.0)
    sums = []
    for s in range(4):
        term = jnp.sum(picked[32 * s : 32 * s + 32] * chosen, axis=0, keepdims=True)
        sums.append(term[:, 0:128] + term[:, 128:256] + term[:, 256:384] + term[:, 384:512])
    nodes = jnp.concatenate(sums + [jnp.zeros((4, 128), F32)], axis=0)
    high, low = split(nodes)
    whigh, wlow = split(jnp.concatenate([wsurf_ref[...], jnp.zeros((4, 512), F32)], axis=0))
    zeros = jnp.zeros((8, 128), BF16)
    lift = contract_first(jnp.concatenate([high, low, high, zeros], axis=0), jnp.concatenate([whigh, whigh, wlow, jnp.zeros((8, 512), BF16)], axis=0))
    atm_in = state_ref[...].astype(F32) + lift
    atm_ref[...] = atm_in
    norm_ref[...] = unit_norm(atm_in, gain_ref[...], 1e-5).astype(BF16)


def front(*args):
    return pl.pallas_call(
        front_kernel,
        out_shape=(
            jax.ShapeDtypeStruct((32, 8, 16, 256), BF16),
            jax.ShapeDtypeStruct((256, 256), BF16),
            jax.ShapeDtypeStruct((128, 512), F32),
            jax.ShapeDtypeStruct((128, 512), BF16),
        ),
        in_specs=[vmem()] * len(args),
        out_specs=tuple([vmem()] * 4),
        compiler_params=pltpu.CompilerParams(vmem_limit_bytes=60 << 20),
        name="front",
    )(*args)


def silu(values):
    return values * jax.nn.sigmoid(values)


def atmosphere_kernel(norm_ref, rims_ref, atm_ref, edges_ref, near_ref, degree_ref, wq_ref, wk_ref, wv_ref, wo_ref, win_ref, wsrc_ref,
                      wdst_ref, wout_ref, wbias_ref, gain_ref, up_ref, down_ref, out_ref, edge_out_ref):
    band = lax.axis_index("comp") * 8 + lax.axis_index("lat")
    col = lax.axis_index("lon")
    ids = near_ref[...]
    part, inside = ids >> 7, ids & 127
    down = (part >> 4) - band
    right = (((part & 15) - col + 1) & 15) - 1
    spot = (down + 1) * 3 + right + 1
    spot = spot - jnp.where(spot > 4, 1, 0)
    at = jnp.where((down == 0) & (right == 0), inside, 128 + spot * 64 + inside)
    info = jnp.concatenate([at, degree_ref[...], degree_ref[...]], axis=0).astype(F32)
    info = info.T
    table = jnp.concatenate([norm_ref[...], rims_ref[...]], axis=0)
    lane = iota((128, 640), 1).astype(F32)
    hots = [jnp.where(lane == info[:, k : k + 1], 1.0, 0.0).astype(BF16) for k in range(6)]
    near = jnp.dot(jnp.concatenate(hots, axis=0), table, preferred_element_type=F32).astype(BF16)
    keys = jnp.dot(near, wk_ref[...], preferred_element_type=F32).astype(BF16)
    values = jnp.dot(near, wv_ref[...], preferred_element_type=F32).astype(BF16)
    far = jnp.dot(near, wdst_ref[...], preferred_element_type=F32).astype(BF16)
    query = jnp.dot(norm_ref[...], wq_ref[...], preferred_element_type=F32).astype(BF16).astype(F32)
    own = jnp.dot(norm_ref[...], wsrc_ref[...], preferred_element_type=F32)
    edges = edges_ref[...].reshape(768, 512)
    before = jnp.dot(edges, win_ref[...], preferred_element_type=F32)
    hidden = []
    for k in range(6):
        rows = slice(128 * k, 128 * k + 128)
        hidden.append(silu(before[rows] + own + far[rows].astype(F32)).astype(BF16))
    edge_sum = edges.astype(F32) + jnp.dot(jnp.concatenate(hidden, axis=0), wout_ref[...], preferred_element_type=F32)
    edge_out_ref[...] = edge_sum.astype(BF16).reshape(6, 128, 512)
    head = jnp.where(iota((8, 512), 0) == iota((8, 512), 1) // 64, 1.0, 0.0)
    scaled = (head * 0.125).astype(BF16)
    bhigh, blow = split(wbias_ref[...])
    mixer = jnp.concatenate([scaled, scaled, bhigh, bhigh, blow], axis=1)
    scores = []
    for k in range(6):
        rows = slice(128 * k, 128 * k + 128)
        qhigh, qlow = split(query * keys[rows].astype(F32))
        ehigh, elow = split(edge_sum[rows])
        score = contract_last(jnp.concatenate([qhigh, qlow, ehigh, elow, ehigh], axis=1), mixer)
        scores.append(jnp.where(info[:, 6:7] > k, score, -1e30))
    most = functools.reduce(jnp.maximum, scores)
    powers = [jnp.exp(score - most) for score in scores]
    total = functools.reduce(jnp.add, powers)
    attended = None
    for k in range(6):
        weight = (powers[k] / total).astype(BF16)
        spread = jnp.dot(weight, head.astype(BF16), preferred_element_type=F32)
        term = spread * values[128 * k : 128 * k + 128].astype(F32)
        attended = term if attended is None else attended + term
    middle = atm_ref[...] + jnp.dot(attended.astype(BF16), wo_ref[...], preferred_element_type=F32)
    normed2 = unit_norm(middle, gain_ref[...], 1e-5).astype(BF16)
    expanded = silu(jnp.dot(normed2, up_ref[...], preferred_element_type=F32)).astype(BF16)
    out_ref[...] = (middle + jnp.dot(expanded, down_ref[...], preferred_element_type=F32)).astype(BF16)


def atmosphere(*args):
    return pl.pallas_call(
        atmosphere_kernel,
        out_shape=(jax.ShapeDtypeStruct((128, 512), BF16), jax.ShapeDtypeStruct((6, 128, 512), BF16)),
        in_specs=[vmem()] * len(args),
        out_specs=(vmem(), vmem()),
        compiler_params=pltpu.CompilerParams(vmem_limit_bytes=60 << 20),
        name="atmosphere",
    )(*args)


def local(atm_state, edge_state, neighbours, degree, surface_fields, ocean_state, wet_mask, flux_columns, flux_weights,
          surface_columns, surface_weights, w_surface, w_flux, ln1_gain, w_query, w_key, w_value, w_out, w_edge_in, w_edge_src,
          w_edge_dst, w_edge_out, w_bias, ln2_gain, w_up, w_down, w_flux_in, dw_kernel, dw_bias, ocean_gain, w_expand, w_reduce,
          layer_scale):
    table = band_gather(atm_state, w_flux.T, surface_fields.reshape(128, 128))
    x, edge, atm_in, normed = front(table, flux_columns, flux_weights, ocean_state, wet_mask, w_flux_in, surface_columns,
                                    surface_weights, atm_state, w_surface, ln1_gain.reshape(1, 512))
    *halo, rims = exchange(x, edge, normed)
    x, edge = ocean_block(False, dw_kernel, dw_bias, ocean_gain, layer_scale, w_expand, w_reduce, wet_mask, x, halo)
    halo = exchange(x, edge)
    ocean_out = ocean_block(True, dw_kernel, dw_bias, ocean_gain, layer_scale, w_expand, w_reduce, wet_mask, x, halo)
    atm_out, edge_out = atmosphere(
        normed, rims.reshape(512, 512), atm_in, edge_state.transpose(1, 0, 2), neighbours.T, degree.reshape(1, 128), w_query, w_key,
        w_value, w_out, w_edge_in, w_edge_src, w_edge_dst, w_edge_out, w_bias.T, ln2_gain.reshape(1, 512), w_up, w_down)
    return atm_out, edge_out.transpose(1, 0, 2), ocean_out


def solution(mesh):
    whole, rows = ("comp", "lat", "lon"), ("comp", "lat")
    in_specs = (
        P(whole, None), P(whole, None, None), P(whole, None), P(whole), P(None, rows, "lon"), P(rows, "lon", None), P(rows, "lon"),
        P(None, rows, "lon"), P(None, rows, "lon"), P(None, whole), P(None, whole)) + (P(),) * 22
    out_specs = (P(whole, None), P(whole, None, None), P(rows, "lon", None))
    return jax.shard_map(local, mesh=mesh, in_specs=in_specs, out_specs=out_specs, check_vma=False)
```

profile of v0, /device:TPU:1, one launch (start us, length us, event | category | flops | bytes accessed | tf_op | source)
XLA Modules:
  0.0 145.3 jit_solution(8771247939693873454)
XLA Ops:
  0.6 24.0 %band_gather.1.table_ref = bf16[16,144,128]{2,1,0:T(8,128)(2,1)} custom-call(bf16[128,512]{1,0:T(8,128)(2,1)} %state_ref.3, f32[4,512]{1,0:T(4,128)} %bitcast.17, f32[128,128]{1,0:T(8,128)} %bitcast.15), custom_call_target="tpu_custom_call" | custom-call | tf_op jit(solution)/shard_map/band_gather/pallas_call | solution.py:270
  24.6 20.6 %front.1 = (bf16[32,8,16,256]{3,2,1,0:T(8,128)(2,1)}, bf16[256,256]{1,0:T(8,128)(2,1)}, f32[128,512]{1,0:T(8,128)}, bf16[128,512]{1,0:T(8,128)(2,1)}) custom-call(bf16[16,144,128]{2,1,0:T(8,128)(2,1)} %band_gather.1.table_ref, s32[4,32,128]{2,1,0:T(8,128)} %cols_ref.1, f32[4,32,128]{2,1,0:T(8,128)} %fluxw_ref.1, bf16[32,128,256]{2,1,0:T(8,128)(2,1)} %ocean_ref.1, ...), custom_call_target="tpu_custom_call" | custom-call | tf_op jit(solution)/shard_map/front/pallas_call | solution.py:418
  45.2 18.4 %exchange_first.1 = (bf16[3,8,16,256]{3,2,1,0:T(8,128)(2,1)}, bf16[3,8,16,256]{3,2,1,0:T(8,128)(2,1)}, bf16[256,256]{1,0:T(8,128)(2,1)}, bf16[256,256]{1,0:T(8,1...) custom-call(bf16[32,8,16,256]{3,2,1,0:T(8,128)(2,1)} %get-tuple-elem, ...), custom_call_target="tpu_custom_call" | custom-call | tf_op jit(solution)/shard_map/exchange_first/pallas_call | solution.py:338
  63.6 10.4 %atmosphere.1 = (bf16[128,512]{1,0:T(8,128)(2,1)}, bf16[6,128,512]{2,1,0:T(8,128)(2,1)}) custom-call(bf16[128,512]{1,0:T(8,128)(2,1)} %get-tuple-element.28.refs_2_.norm_ref, bf16[512,512]{1,0:T(8,128)(2,1)} %bitcast.12, f32[128,512]{1,0:T(8,128)} %get-tuple-element.32.atm_ref, bf16[6,128,512]{2,1,0:T(8,128)(2,1)} %bitcast.11, s32[6,128]{1,0:T(8,128)} %bitcast.18, ...), custom_call_target="tpu_custom_call" | custom-call | tf_op jit(solution)/shard_map/atmosphere/pallas_call | solution.py:494
  74.0 28.7 %ocean_first.1 = (bf16[32,8,16,256]{3,2,1,0:T(8,128)(2,1)}, bf16[256,256]{1,0:T(8,128)(2,1)}) custom-call(f32[49,2,256]{2,1,0:T(2,128)} %bitcast.13, f32[2,256]{1,0:T(2,128)} %refs_1_.3, f32[2,256]{1,0:T(2,128)} %refs_2_.3, f32[2,256]{1,0:T(2,128)} %refs_3_.3, bf16[2,256,1024]{2,1,0:T(8,128)(2,1)} %refs_4_.3, bf16[2,1024,256]{2,1,0:T(8,128)(2,1)} %refs_5_.3, ...), custom_call_target="tpu_custom_call" | custom-call | tf_op jit(solution)/shard_map/ocean_first/pallas_call | solution.py:200
  102.7 13.3 %exchange_second.1 = (bf16[3,8,16,256]{3,2,1,0:T(8,128)(2,1)}, bf16[3,8,16,256]{3,2,1,0:T(8,128)(2,1)}, bf16[256,256]{1,0:T(8,128)(2,1)}, bf16[256,256]{1,0:T(8,...) custom-call(bf16[32,8,16,256]{3,2,1,0:T(8,128)(2,1)} %get-tuple-elem, ...), custom_call_target="tpu_custom_call" | custom-call | tf_op jit(solution)/shard_map/exchange_second/pallas_call | solution.py:338
  116.0 29.4 %ocean_last.1 = bf16[32,128,256]{2,1,0:T(8,128)(2,1)} custom-call(f32[49,2,256]{2,1,0:T(2,128)} %bitcast.14, f32[2,256]{1,0:T(2,128)} %refs_1_.3, f32[2,256]{1,0:T(2,128)} %refs_2_.3, f32[2,256]{1,0:T(2,128)} %refs_3_.3, bf16[2,256,1024]{2,1,0:T(8,128)(2,1)} %refs_4_.3, bf16[2,1024,256]{2,1,0:T(8,128)(2,1)} %refs_5_.3, s32[32,128]{1,0:T(8,128)} %refs_6_.3, ...), custom_call_target="tpu_custom_call" | custom-call | tf_op jit(solution)/shard_map/ocean_last/pallas_call | solution.py:200
where the time goes:
time: 145 us
  Pallas kernels  145 us (100%)
    pallas_call x2, Pallas kernels, ocean_block(): pl.pallas_call(body, out_shape=shapes, in_specs=specs_in, out_specs=specs...  58.1 us
    pallas_call x2, Pallas kernels, exchange(): pl.pallas_call(functools.partial(halo_kernel, rims), out_shape=tuple(shap...  31.6 us
    pallas_call x1, Pallas kernels, band_gather(): pl.pallas_call(gather_kernel, out_shape=jax.ShapeDtypeStruct((16, 144, 12...  24 us
    pallas_call x1, Pallas kernels, front(): pl.pallas_call(front_kernel, out_shape=(jax.ShapeDtypeStruct((32, 8, 16,...  20.6 us
    pallas_call x1, Pallas kernels, atmosphere(): pl.pallas_call(atmosphere_kernel, out_shape=(jax.ShapeDtypeStruct((128, 5...  10.4 us

commit v1 on v0

--- a/solution.py
+++ b/solution.py
@@ -65,14 +65,14 @@
         if p < 3:
             data = plain[p + 5]
             one_view[p] = data
-            edge = jnp.broadcast_to(west[p + 4 : p + 5], (16, 256))
+            edge = jnp.broadcast_to(west(p), (16, 256))
             zero_view[p] = jnp.where(first, edge, pltpu.roll(data.astype(F32), 1, 0)).astype(BF16)
         else:
             data = plain[p - 3]
             zero_view[p] = data
             rolled = pltpu.roll(data.astype(F32), 15, 0)
             if p < 6:
-                rolled = jnp.where(last, jnp.broadcast_to(east[p - 3 : p - 2], (16, 256)), rolled)
+                rolled = jnp.where(last, jnp.broadcast_to(east(p - 3), (16, 256)), rolled)
             one_view[p] = rolled.astype(BF16)
     for q, view in enumerate((zero_view, one_view)):
         for t in range(2):
@@ -82,20 +82,29 @@
                     xt_ref[q, 4 * t + u, row, :, 128 * h : 128 * h + 128] = done[u]
 
 
-def block_body(last, kernel_ref, bias_ref, gain_ref, scale_ref, up_ref, down_ref, mask_ref, x_ref, north_ref, south_ref,
-               west_ref, east_ref, nw_ref, ne_ref, sw_ref, se_ref, out_ref, edge_ref, w_ref, xt_ref, conv_ref, stat_ref, rms_ref):
+def block_body(last, kernel_ref, bias_ref, gain_ref, scale_ref, up_ref, down_ref, mask_ref, x_ref, arrived, halo,
+               out_ref, edge_ref, w_ref, xt_ref, conv_ref, stat_ref, rms_ref, side_ref, corner_ref, lines_ref):
     block = 1 if last else 0
     build_weights(block, kernel_ref, w_ref)
+    arrived()
+    north_ref, south_ref, west_ref, east_ref, nw_ref, ne_ref, sw_ref, se_ref = halo
+    side_ref[0:3] = west_ref[...].astype(F32)
+    side_ref[3:6] = east_ref[...].astype(F32)
+    for n, ref in enumerate((nw_ref, ne_ref, sw_ref, se_ref)):
+        corner_ref[3 * n : 3 * n + 3] = ref[...].astype(F32)
 
     def interior(r, carry):
-        at = pl.multiple_of(r * 8, 8)
-        fill_rows(lambda j: x_ref[r, j], west_ref[pl.ds(at, 8)].astype(F32), east_ref[pl.ds(at, 8)].astype(F32), xt_ref, r + 3)
+        fill_rows(lambda j: x_ref[r, j], lambda p: side_ref[p, pl.ds(r, 1)], lambda p: side_ref[3 + p, pl.ds(r, 1)], xt_ref, r + 3)
         return carry
 
     lax.fori_loop(0, 32, interior, 0, unroll=2)
-    for k in range(3):
-        fill_rows(lambda j: north_ref[k, j], nw_ref[8 + 8 * k : 16 + 8 * k].astype(F32), ne_ref[8 + 8 * k : 16 + 8 * k].astype(F32), xt_ref, k)
-        fill_rows(lambda j: south_ref[k, j], sw_ref[8 * k : 8 * k + 8].astype(F32), se_ref[8 * k : 8 * k + 8].astype(F32), xt_ref, 35 + k)
+
+    def outer(k, carry):
+        fill_rows(lambda j: north_ref[k, j], lambda p: corner_ref[p, pl.ds(13 + k, 1)], lambda p: corner_ref[3 + p, pl.ds(13 + k, 1)], xt_ref, k)
+        fill_rows(lambda j: south_ref[k, j], lambda p: corner_ref[6 + p, pl.ds(k, 1)], lambda p: corner_ref[9 + p, pl.ds(k, 1)], xt_ref, 35 + k)
+        return carry
+
+    lax.fori_loop(0, 3, outer, 0)
 
     grouped = []
     lines = jnp.concatenate([bias_ref[block : block + 1]] + [gain_ref[block : block + 1]] * 7, axis=0)
@@ -165,53 +174,18 @@
                 out_ref[4 * n + k] = natural.astype(BF16)
         else:
             out_ref[pl.ds(4 * n, 4)] = fresh16.reshape(4, 8, 16, 256)
-            lines = []
             for k in range(4):
-                lines += edge_lines(fresh[128 * k : 128 * k + 128])
-            edge_ref[pl.ds(pl.multiple_of(32 * n, 32), 32)] = jnp.concatenate(lines, axis=0).astype(BF16)
+                keep_edges(lines_ref, 4 * n + k, fresh[128 * k : 128 * k + 128], (0, 16, 32, 95, 111, 127))
         return carry
 
     lax.fori_loop(0, 8, mlp, 0, unroll=2)
-
-
-def edge_lines(rows):
-    at = (0, 16, 32, 48, 95, 111, 127, 111)
-    return [rows[p : p + 1] for p in at]
-
-
-def ocean_block(last, kernel, bias, gain, scale, up, down, mask, x, halo):
-    def body(*refs):
-        ins, rest = refs[:16], refs[16:]
-        if last:
-            out_ref, scratch = rest[0], rest[1:]
-            block_body(True, *ins, out_ref, None, *scratch)
-        else:
-            block_body(False, *ins, rest[0], rest[1], *rest[2:])
-
-    vm = pl.BlockSpec(memory_space=pltpu.VMEM)
-    args = (kernel.transpose(1, 0, 2), bias, gain, scale, up, down, mask, x) + tuple(halo)
-    specs_in = [vm] * len(args)
-    if last:
-        shapes = jax.ShapeDtypeStruct((32, 128, 256), BF16)
-        specs = vm
-    else:
-        shapes = (jax.ShapeDtypeStruct((32, 8, 16, 256), BF16), jax.ShapeDtypeStruct((256, 256), BF16))
-        specs = (vm, vm)
-    return pl.pallas_call(
-        body,
-        out_shape=shapes,
-        in_specs=specs_in,
-        out_specs=specs,
-        scratch_shapes=[
-            pltpu.VMEM((8, 3584, 256), BF16),
-            pltpu.VMEM((2, 8, 38, 16, 256), BF16),
-            pltpu.VMEM((8, 512, 256), F32),
-            pltpu.VMEM((512, 256), F32),
-            pltpu.VMEM((512, 256), F32),
-        ],
-        compiler_params=pltpu.CompilerParams(vmem_limit_bytes=60 << 20),
-        name="ocean_last" if last else "ocean_first",
-    )(*args)
+    if not last:
+        edge_ref[...] = lines_ref[...].astype(BF16)
+
+
+def keep_edges(lines_ref, r, rows, at):
+    for n, p in enumerate(at):
+        lines_ref[n, pl.ds(r, 1)] = rows[p : p + 1]
 
 
 def vmem():
@@ -241,116 +215,128 @@
     return centre * lax.rsqrt(spread + epsilon) * gain
 
 
-def gather_kernel(state_ref, wflux_ref, fields_ref, table_ref, own_ref, send_sem, recv_sem, local_sem):
+AROUND = [(dr, dc) for dr in (-1, 0, 1) for dc in (-1, 0, 1) if (dr, dc) != (0, 0)]
+HALO = [((3, 8, 16, 256), BF16)] * 2 + [((3, 32, 256), BF16)] * 2 + [((3, 16, 256), BF16)] * 4
+BLOCK_SCRATCH = [
+    ((8, 3584, 256), BF16), ((2, 8, 38, 16, 256), BF16), ((8, 512, 256), F32), ((512, 256), F32), ((512, 256), F32),
+    ((6, 32, 256), F32), ((12, 16, 256), F32), ((6, 32, 256), F32)]
+
+
+def greet(devices):
+    barrier = pltpu.get_barrier_semaphore()
+    for device in devices:
+        pl.semaphore_signal(barrier, inc=1, device_id=device, device_id_type=pl.DeviceIdType.MESH)
+    pl.semaphore_wait(barrier, len(devices))
+
+
+def neighbour(dr, dc):
+    band = lax.axis_index("comp") * 8 + lax.axis_index("lat")
+    row = lax.rem(band + 16 + dr, 16)
+    return {"comp": row // 8, "lat": lax.rem(row, 8), "lon": lax.rem(lax.axis_index("lon") + 16 + dc, 16)}
+
+
+def send(source, target, send_sem, recv_sem, device):
+    copy = pltpu.make_async_remote_copy(
+        src_ref=source, dst_ref=target, send_sem=send_sem, recv_sem=recv_sem, device_id=device, device_id_type=pl.DeviceIdType.MESH)
+    copy.start()
+    return copy
+
+
+def start_halo(x_ref, edge_ref, halo, send_sem, recv_sem):
+    north, south, west, east, nw, ne, sw, se = halo
+    left, right = edge_ref.at[pl.ds(0, 3)], edge_ref.at[pl.ds(3, 3)]
+    top, bottom = pl.ds(0, 16), pl.ds(16, 16)
+    moves = [
+        (x_ref.at[pl.ds(0, 3)], south, -1, 0), (x_ref.at[pl.ds(29, 3)], north, 1, 0), (left, east, 0, -1), (right, west, 0, 1),
+        (edge_ref.at[pl.ds(0, 3), top], se, -1, -1), (edge_ref.at[pl.ds(3, 3), top], sw, -1, 1),
+        (edge_ref.at[pl.ds(0, 3), bottom], ne, 1, -1), (edge_ref.at[pl.ds(3, 3), bottom], nw, 1, 1)]
+    return [
+        send(source, target, send_sem.at[n], recv_sem.at[n], neighbour(dr, dc))
+        for n, (source, target, dr, dc) in enumerate(moves)]
+
+
+def first_kernel(*refs):
+    ins, x_ref, edge_ref, norm_ref = refs[:7], refs[7], refs[8], refs[9]
+    out_ref, line_ref, rims_ref = refs[10:13]
+    scratch, halo = refs[13:21], refs[21:29]
+    send_sem, recv_sem = refs[29], refs[30]
+    greet([neighbour(dr, dc) for dr, dc in AROUND])
+    copies = start_halo(x_ref, edge_ref, halo, send_sem, recv_sem)
+    rims = []
+    for n, (dr, dc) in enumerate(AROUND):
+        slot = (1 - dr) * 3 + 1 - dc
+        slot = slot - 1 if slot > 4 else slot
+        rims.append(send(norm_ref.at[pl.ds(0, 64)], rims_ref.at[slot], send_sem.at[8 + n], recv_sem.at[8 + n], neighbour(dr, dc)))
+
+    def arrived():
+        for copy in copies:
+            copy.wait()
+
+    block_body(False, *ins, x_ref, arrived, halo, out_ref, line_ref, *scratch)
+    for copy in rims:
+        copy.wait()
+
+
+def ocean_first(*args):
+    scratch = [pltpu.VMEM(*item) for item in BLOCK_SCRATCH + HALO] + [pltpu.SemaphoreType.DMA((16,))] * 2
+    return pl.pallas_call(
+        first_kernel,
+        out_shape=(
+            jax.ShapeDtypeStruct((32, 8, 16, 256), BF16), jax.ShapeDtypeStruct((6, 32, 256), BF16),
+            jax.ShapeDtypeStruct((8, 64, 512), BF16)),
+        in_specs=[vmem()] * len(args),
+        out_specs=(vmem(), vmem(), anywhere()),
+        scratch_shapes=scratch,
+        compiler_params=pltpu.CompilerParams(vmem_limit_bytes=60 << 20, collective_id=1, has_side_effects=True),
+        name="ocean_first",
+    )(*args)
+
+
+def last_kernel(*refs):
+    ins, x_ref, halo, out_ref, scratch = refs[:7], refs[7], refs[8:16], refs[16], refs[17:]
+    block_body(True, *ins, x_ref, lambda: None, halo, out_ref, None, *scratch)
+
+
+def ocean_last(*args):
+    return pl.pallas_call(
+        last_kernel,
+        out_shape=jax.ShapeDtypeStruct((32, 128, 256), BF16),
+        in_specs=[vmem()] * len(args),
+        out_specs=vmem(),
+        scratch_shapes=[pltpu.VMEM(*item) for item in BLOCK_SCRATCH],
+        compiler_params=pltpu.CompilerParams(vmem_limit_bytes=60 << 20),
+        name="ocean_last",
+    )(*args)
+
+
+def front_kernel(wflux_ref, fields_ref, cols_ref, fluxw_ref, ocean_ref, mask_ref, wfin_ref, scols_ref, sw_ref, state_ref, wsurf_ref,
+                 gain_ref, x_ref, edge_ref, atm_ref, norm_ref, flux_own, field_own, flux_tab, field_tab, lines_ref,
+                 flux_send, flux_recv, field_send, field_recv, pass_send, pass_recv):
     me = lax.axis_index("lon")
+    side, deep = me // 8, lax.rem(me, 8)
+    partner = {"lon": lax.rem(me + 8, 16)}
     high, low = split(wflux_ref[...])
     both = contract_last(jnp.concatenate([high, low], axis=0), state_ref[...])
-    fluxes = both[0:4] + both[4:8]
-    own_ref[0:128] = fields_ref[...].astype(BF16)
-    own_ref[128:144] = jnp.concatenate([fluxes, jnp.zeros((12, 128), F32)], axis=0).astype(BF16)
-    barrier = pltpu.get_barrier_semaphore()
-    for step in range(1, 16):
-        pl.semaphore_signal(barrier, inc=1, device_id={"lon": lax.rem(me + step, 16)}, device_id_type=pl.DeviceIdType.MESH)
-    pl.semaphore_wait(barrier, 15)
-    copies = []
-    for step in range(1, 16):
-        copy = pltpu.make_async_remote_copy(
-            src_ref=own_ref, dst_ref=table_ref.at[me], send_sem=send_sem.at[step], recv_sem=recv_sem.at[step],
-            device_id={"lon": lax.rem(me + step, 16)}, device_id_type=pl.DeviceIdType.MESH)
-        copy.start()
-        copies.append(copy)
-    mine = pltpu.make_async_copy(own_ref, table_ref.at[me], local_sem)
-    mine.start()
-    mine.wait()
-    for copy in copies:
+    fluxes = jnp.concatenate([both[0:4] + both[4:8], jnp.zeros((12, 128), F32)], axis=0).astype(BF16)
+    fields = fields_ref[...].astype(BF16)
+    flux_own[...] = fluxes
+    field_own[...] = fields
+    flux_tab[me] = fluxes
+    field_tab[me] = fields
+    greet([{"lon": lax.rem(me + step, 16)} for step in range(1, 16)])
+    small_copies = [
+        send(flux_own, flux_tab.at[me], flux_send.at[step], flux_recv.at[step], {"lon": lax.rem(me + step, 16)})
+        for step in range(1, 16)]
+    field_copies = [
+        send(field_own, field_tab.at[me], field_send.at[step], field_recv.at[step], {"lon": side * 8 + lax.rem(deep + step, 8)})
+        for step in range(1, 8)]
+    pass_copies = [send(field_own, field_tab.at[me], pass_send.at[0], pass_recv.at[0], partner)]
+    for copy in small_copies:
         copy.wait()
 
-
-def band_gather(state, wflux, fields):
-    return pl.pallas_call(
-        gather_kernel,
-        out_shape=jax.ShapeDtypeStruct((16, 144, 128), BF16),
-        in_specs=[vmem()] * 3,
-        out_specs=anywhere(),
-        scratch_shapes=[pltpu.VMEM((144, 128), BF16), pltpu.SemaphoreType.DMA((16,)), pltpu.SemaphoreType.DMA((16,)), pltpu.SemaphoreType.DMA],
-        compiler_params=pltpu.CompilerParams(collective_id=0, has_side_effects=True),
-        name="band_gather",
-    )(state, wflux, fields)
-
-
-def halo_kernel(with_rims, *refs):
-    if with_rims:
-        x_ref, edge_ref, norm_ref = refs[:3]
-        rims_ref = refs[11]
-        halo, send_sem, recv_sem = refs[3:11], refs[12], refs[13]
-    else:
-        x_ref, edge_ref = refs[:2]
-        halo, send_sem, recv_sem = refs[2:10], refs[10], refs[11]
-    north, south, west, east, nw, ne, sw, se = halo
-    band = lax.axis_index("comp") * 8 + lax.axis_index("lat")
-    col = lax.axis_index("lon")
-
-    def device(dr, dc):
-        row = lax.rem(band + 16 + dr, 16)
-        return {"comp": row // 8, "lat": lax.rem(row, 8), "lon": lax.rem(col + 16 + dc, 16)}
-
-    around = [(dr, dc) for dr in (-1, 0, 1) for dc in (-1, 0, 1) if (dr, dc) != (0, 0)]
-    barrier = pltpu.get_barrier_semaphore()
-    for dr, dc in around:
-        pl.semaphore_signal(barrier, inc=1, device_id=device(dr, dc), device_id_type=pl.DeviceIdType.MESH)
-    pl.semaphore_wait(barrier, 8)
-    top, bottom = edge_ref.at[pl.ds(0, 32)], edge_ref.at[pl.ds(224, 32)]
-    moves = [
-        (x_ref.at[pl.ds(0, 3)], south, -1, 0),
-        (x_ref.at[pl.ds(29, 3)], north, 1, 0),
-        (edge_ref, east, 0, -1),
-        (edge_ref, west, 0, 1),
-        (top, se, -1, -1),
-        (top, sw, -1, 1),
-        (bottom, ne, 1, -1),
-        (bottom, nw, 1, 1),
-    ]
-    if with_rims:
-        for dr, dc in around:
-            slot = (1 - dr) * 3 + 1 - dc
-            slot = slot - 1 if slot > 4 else slot
-            moves.append((norm_ref.at[pl.ds(0, 64)], rims_ref.at[slot], dr, dc))
-    copies = []
-    for n, (source, target, dr, dc) in enumerate(moves):
-        copy = pltpu.make_async_remote_copy(
-            src_ref=source, dst_ref=target, send_sem=send_sem.at[n], recv_sem=recv_sem.at[n],
-            device_id=device(dr, dc), device_id_type=pl.DeviceIdType.MESH)
-        copy.start()
-        copies.append(copy)
-    for copy in copies:
-        copy.wait()
-
-
-def exchange(x, edge, normed=None):
-    rims = normed is not None
-    shapes = [jax.ShapeDtypeStruct((3, 8, 16, 256), BF16)] * 2 + [jax.ShapeDtypeStruct((256, 256), BF16)] * 2
-    shapes += [jax.ShapeDtypeStruct((32, 256), BF16)] * 4
-    args = [x, edge]
-    if rims:
-        shapes.append(jax.ShapeDtypeStruct((8, 64, 512), BF16))
-        args.append(normed)
-    count = 16 if rims else 8
-    return pl.pallas_call(
-        functools.partial(halo_kernel, rims),
-        out_shape=tuple(shapes),
-        in_specs=[anywhere()] * len(args),
-        out_specs=tuple([anywhere()] * len(shapes)),
-        scratch_shapes=[pltpu.SemaphoreType.DMA((count,)), pltpu.SemaphoreType.DMA((count,))],
-        compiler_params=pltpu.CompilerParams(collective_id=1 if rims else 2, has_side_effects=True),
-        name="exchange_first" if rims else "exchange_second",
-    )(*args)
-
-
-def front_kernel(table_ref, cols_ref, fluxw_ref, ocean_ref, mask_ref, wfin_ref, scols_ref, sw_ref, state_ref, wsurf_ref, gain_ref,
-                 x_ref, edge_ref, atm_ref, norm_ref):
     pairs = []
     for p in range(8):
-        pairs.append(jnp.concatenate([table_ref[2 * p, 128:132], table_ref[2 * p + 1, 128:132]], axis=0))
+        pairs.append(jnp.concatenate([flux_tab[2 * p, 0:4], flux_tab[2 * p + 1, 0:4]], axis=0))
     small = jnp.concatenate(pairs, axis=0)
     node = iota((128, 128), 0)
     half = iota((8, 128), 0) // 4
@@ -383,11 +369,18 @@
         fresh = both[:, 256:512] * (ocean_ref[r].astype(F32) + both[:, 0:256])
         fresh16 = fresh.astype(BF16)
         x_ref[r] = jnp.dot(order, fresh16, preferred_element_type=F32).astype(BF16).reshape(8, 16, 256)
-        line = jnp.concatenate([fresh[0:4], fresh[125:128], fresh[127:128]], axis=0)
-        edge_ref[pl.ds(pl.multiple_of(r * 8, 8), 8)] = line.astype(BF16)
+        keep_edges(lines_ref, r, fresh, (0, 1, 2, 125, 126, 127))
         return carry
 
-    lax.fori_loop(0, 32, row, 0)
+    lax.fori_loop(0, 16, row, 0, unroll=2)
+    for step in range(1, 8):
+        field_copies[step - 1].wait()
+        block = field_tab.at[side * 8 + lax.rem(deep + 8 - step, 8)]
+        pass_copies.append(send(block, block, pass_send.at[step], pass_recv.at[step], partner))
+    lax.fori_loop(16, 32, row, 0, unroll=2)
+    edge_ref[...] = lines_ref[...].astype(BF16)
+    for copy in pass_copies:
+        copy.wait()
 
     ids = jnp.concatenate([scols_ref[k : k + 1] for k in range(4)], axis=1)
     cell = ids & 2047
@@ -396,7 +389,7 @@
     hots, tabs = [], []
     for p in range(16):
         hots.append(jnp.where(spot + 128 * p == cell, 1.0, 0.0).astype(BF16))
-        tabs.append(table_ref[p, 0:128])
+        tabs.append(field_tab[p])
     picked = jnp.dot(jnp.concatenate(tabs, axis=1), jnp.concatenate(hots, axis=0), preferred_element_type=F32)
     weight = jnp.concatenate([sw_ref[k : k + 1] for k in range(4)], axis=1)
     chosen = jnp.where(iota((32, 512), 0) == level, weight, 0.0)
@@ -419,13 +412,16 @@
         front_kernel,
         out_shape=(
             jax.ShapeDtypeStruct((32, 8, 16, 256), BF16),
-            jax.ShapeDtypeStruct((256, 256), BF16),
+            jax.ShapeDtypeStruct((6, 32, 256), BF16),
             jax.ShapeDtypeStruct((128, 512), F32),
             jax.ShapeDtypeStruct((128, 512), BF16),
         ),
         in_specs=[vmem()] * len(args),
         out_specs=tuple([vmem()] * 4),
-        compiler_params=pltpu.CompilerParams(vmem_limit_bytes=60 << 20),
+        scratch_shapes=[
+            pltpu.VMEM((16, 128), BF16), pltpu.VMEM((128, 128), BF16), pltpu.VMEM((16, 16, 128), BF16), pltpu.VMEM((16, 128, 128), BF16),
+            pltpu.VMEM((6, 32, 256), F32)] + [pltpu.SemaphoreType.DMA((16,))] * 2 + [pltpu.SemaphoreType.DMA((8,))] * 4,
+        compiler_params=pltpu.CompilerParams(vmem_limit_bytes=60 << 20, collective_id=0, has_side_effects=True),
         name="front",
     )(*args)
 
@@ -435,7 +431,9 @@
 
 
 def atmosphere_kernel(norm_ref, rims_ref, atm_ref, edges_ref, near_ref, degree_ref, wq_ref, wk_ref, wv_ref, wo_ref, win_ref, wsrc_ref,
-                      wdst_ref, wout_ref, wbias_ref, gain_ref, up_ref, down_ref, out_ref, edge_out_ref):
+                      wdst_ref, wout_ref, wbias_ref, gain_ref, up_ref, down_ref, x_ref, line_ref, out_ref, edge_out_ref, *rest):
+    greet([neighbour(dr, dc) for dr, dc in AROUND])
+    copies = start_halo(x_ref, line_ref, rest[:8], rest[8], rest[9])
     band = lax.axis_index("comp") * 8 + lax.axis_index("lat")
     col = lax.axis_index("lon")
     ids = near_ref[...]
@@ -488,15 +486,19 @@
     normed2 = unit_norm(middle, gain_ref[...], 1e-5).astype(BF16)
     expanded = silu(jnp.dot(normed2, up_ref[...], preferred_element_type=F32)).astype(BF16)
     out_ref[...] = (middle + jnp.dot(expanded, down_ref[...], preferred_element_type=F32)).astype(BF16)
+    for copy in copies:
+        copy.wait()
 
 
 def atmosphere(*args):
     return pl.pallas_call(
         atmosphere_kernel,
-        out_shape=(jax.ShapeDtypeStruct((128, 512), BF16), jax.ShapeDtypeStruct((6, 128, 512), BF16)),
-        in_specs=[vmem()] * len(args),
-        out_specs=(vmem(), vmem()),
-        compiler_params=pltpu.CompilerParams(vmem_limit_bytes=60 << 20),
+        out_shape=(jax.ShapeDtypeStruct((128, 512), BF16), jax.ShapeDtypeStruct((6, 128, 512), BF16))
+        + tuple(jax.ShapeDtypeStruct(*item) for item in HALO),
+        in_specs=[vmem()] * (len(args) - 2) + [anywhere()] * 2,
+        out_specs=(vmem(), vmem()) + (anywhere(),) * 8,
+        scratch_shapes=[pltpu.SemaphoreType.DMA((8,))] * 2,
+        compiler_params=pltpu.CompilerParams(vmem_limit_bytes=60 << 20, collective_id=2, has_side_effects=True),
         name="atmosphere",
     )(*args)
 
@@ -505,16 +507,15 @@
           surface_columns, surface_weights, w_surface, w_flux, ln1_gain, w_query, w_key, w_value, w_out, w_edge_in, w_edge_src,
           w_edge_dst, w_edge_out, w_bias, ln2_gain, w_up, w_down, w_flux_in, dw_kernel, dw_bias, ocean_gain, w_expand, w_reduce,
           layer_scale):
-    table = band_gather(atm_state, w_flux.T, surface_fields.reshape(128, 128))
-    x, edge, atm_in, normed = front(table, flux_columns, flux_weights, ocean_state, wet_mask, w_flux_in, surface_columns,
-                                    surface_weights, atm_state, w_surface, ln1_gain.reshape(1, 512))
-    *halo, rims = exchange(x, edge, normed)
-    x, edge = ocean_block(False, dw_kernel, dw_bias, ocean_gain, layer_scale, w_expand, w_reduce, wet_mask, x, halo)
-    halo = exchange(x, edge)
-    ocean_out = ocean_block(True, dw_kernel, dw_bias, ocean_gain, layer_scale, w_expand, w_reduce, wet_mask, x, halo)
-    atm_out, edge_out = atmosphere(
+    x, edge, atm_in, normed = front(
+        w_flux.T, surface_fields.reshape(128, 128), flux_columns, flux_weights, ocean_state, wet_mask, w_flux_in, surface_columns,
+        surface_weights, atm_state, w_surface, ln1_gain.reshape(1, 512))
+    ocean = (dw_kernel.transpose(1, 0, 2), dw_bias, ocean_gain, layer_scale, w_expand, w_reduce, wet_mask)
+    x, edge, rims = ocean_first(*ocean, x, edge, normed)
+    atm_out, edge_out, *halo = atmosphere(
         normed, rims.reshape(512, 512), atm_in, edge_state.transpose(1, 0, 2), neighbours.T, degree.reshape(1, 128), w_query, w_key,
-        w_value, w_out, w_edge_in, w_edge_src, w_edge_dst, w_edge_out, w_bias.T, ln2_gain.reshape(1, 512), w_up, w_down)
+        w_value, w_out, w_edge_in, w_edge_src, w_edge_dst, w_edge_out, w_bias.T, ln2_gain.reshape(1, 512), w_up, w_down, x, edge)
+    ocean_out = ocean_last(*ocean, x, *halo)
     return atm_out, edge_out.transpose(1, 0, 2), ocean_out
 
 

time: 145 us -> 121 us (0.83)
  Pallas kernels: 145 us -> 119 us
  local copies, waits for them, and re-layouts: 0 us -> 1.54 us
    pallas_call x5 -> x2, Pallas kernels: 114 us -> 69.4 us  [the longest x1 39.4 us: ocean_first(): pl.pallas_call(first_kernel, out_shape=(jax.ShapeDtypeStruct((32, 8, 16,...]
    pallas_call x1, Pallas kernels: 20.6 us -> 31.5 us  [front(): pl.pallas_call(front_kernel, out_shape=(jax.ShapeDtypeStruct((32, 8, 16,...]
    pallas_call x1, Pallas kernels: 10.4 us -> 17.9 us  [atmosphere(): pl.pallas_call(atmosphere_kernel, out_shape=(jax.ShapeDtypeStruct((128, 5...]
    unnamed x0 -> x6, local copies, waits for them, and re-layouts: none -> 1.54 us
where the time goes in v1:
time: 121 us
  Pallas kernels  119 us (98%)
  local copies, waits for them, and re-layouts  1.54 us (1%)
    pallas_call x1, Pallas kernels, ocean_first(): pl.pallas_call(first_kernel, out_shape=(jax.ShapeDtypeStruct((32, 8, 16,...  39.4 us
    pallas_call x1, Pallas kernels, front(): pl.pallas_call(front_kernel, out_shape=(jax.ShapeDtypeStruct((32, 8, 16,...  31.5 us
    pallas_call x1, Pallas kernels, ocean_last(): pl.pallas_call(last_kernel, out_shape=jax.ShapeDtypeStruct((32, 128, 256)...  30.1 us
    pallas_call x1, Pallas kernels, atmosphere(): pl.pallas_call(atmosphere_kernel, out_shape=(jax.ShapeDtypeStruct((128, 5...  17.9 us

profile of v1, /device:TPU:1, one launch (start us, length us, event | category | flops | bytes accessed | tf_op | source)
XLA Modules:
  0.0 121.1 jit_solution(16004401639420573423)
XLA Ops:
  0.6 31.5 %front.1 = (bf16[32,8,16,256]{3,2,1,0:T(8,128)(2,1)}, bf16[6,32,256]{2,1,0:T(8,128)(2,1)}, f32[128,512]{1,0:T(8,128)}, bf16[128,512]{1,0:T(8,128)(2,1)}) custom-call(f32[4,512]{1,0:T(4,128)} %bitcast.18, f32[128,128]{1,0:T(8,128)} %bitcast.16, s32[4,32,128]{2,1,0:T(8,128)} %cols_ref.1, f32[4,32,128]{2,1,0:T(8,128)} %fluxw_ref.1, ...), custom_call_target="tpu_custom_call" | custom-call | tf_op jit(solution)/shard_map/front/pallas_call | solution.py:411
  32.2 39.4 %ocean_first.1 = (bf16[32,8,16,256]{3,2,1,0:T(8,128)(2,1)}, bf16[6,32,256]{2,1,0:T(8,128)(2,1)}, bf16[8,64,512]{2,1,0:T(8,128)(2,1)}) custom-call(f32[49,2,256]{2,1,0:T(2,128)} %bitcast.14, f32[2,256]{1,0:T(2,128)} %refs_1_.3, f32[2,256]{1,0:T(2,128)} %refs_2_.3, f32[2,256]{1,0:T(2,128)} %refs_3_.3, bf16[2,256,1024]{2,1,0:T(8,128)(2,1)} %refs_4_.3, ...), custom_call_target="tpu_custom_call" | custom-call | tf_op jit(solution)/shard_map/ocean_first/pallas_call | solution.py:282
  71.6 17.9 %atmosphere.1 = (bf16[128,512]{1,0:T(8,128)(2,1)}, bf16[6,128,512]{2,1,0:T(8,128)(2,1)}, bf16[3,8,16,256]{3,2,1,0:T(8,128)(2,1)}, bf16[3,8,16,256]{3,2,1,0:T(8,1...) custom-call(bf16[128,512]{1,0:T(8,128)(2,1)} %get-tuple-element.20.r, ...), custom_call_target="tpu_custom_call" | custom-call | tf_op jit(solution)/shard_map/atmosphere/pallas_call | solution.py:494
  89.5 0.0 copy-start.1
  89.5 0.0 copy-start
  89.5 30.1 %ocean_last.1 = bf16[32,128,256]{2,1,0:T(8,128)(2,1)} custom-call(f32[49,2,256]{2,1,0:T(2,128)} %bitcast.15, f32[2,256]{1,0:T(2,128)} %refs_1_.3, f32[2,256]{1,0:T(2,128)} %refs_2_.3, f32[2,256]{1,0:T(2,128)} %refs_3_.3, bf16[2,256,1024]{2,1,0:T(8,128)(2,1)} %refs_4_.3, bf16[2,1024,256]{2,1,0:T(8,128)(2,1)} %refs_5_.3, s32[32,128]{1,0:T(8,128)} %refs_6_.3, ...), custom_call_target="tpu_custom_call" | custom-call | tf_op jit(solution)/shard_map/ocean_last/pallas_call | solution.py:301
  119.6 0.0 copy-done.1
  119.6 0.7 copy.38
  120.2 0.0 copy-done
  120.2 0.9 copy.39
Async XLA Ops:
  89.5 30.1 %copy-start.1 = (bf16[128,512]{1,0:T(8,128)(2,1)S(1)}, bf16[128,512]{1,0:T(8,128)(2,1)}, u32[]{:S(2)}) copy-start(bf16[128,512]{1,0:T(8,128)(2,1)} %get-tuple-element.40) | copy-start | bytes 393220
  89.5 30.7 %copy-start = (bf16[6,128,512]{2,1,0:T(8,128)(2,1)S(1)}, bf16[6,128,512]{2,1,0:T(8,128)(2,1)}, u32[]{:S(2)}) copy-start(bf16[6,128,512]{2,1,0:T(8,128)(2,1)} %get-tuple-element.28) | copy-start | bytes 2359300

commit v2 on v1

--- a/solution.py
+++ b/solution.py
@@ -36,7 +36,7 @@
 
 
 def build_weights(block, kernel_ref, w_ref):
-    eye = (iota((32, 256), 0) == iota((32, 256), 1) % 32)
+    eye = jnp.where(iota((32, 256), 0) == iota((32, 256), 1) % 32, 1.0, 0.0).astype(BF16)
 
     def body(tap, carry):
         rows = kernel_ref[pl.ds(tap * 7, 7), block]
@@ -49,66 +49,55 @@
             for u in range(4):
                 line = jnp.concatenate([halves[0][u], halves[1][u]], axis=1)
                 for n in range(16):
-                    piece = jnp.where(eye, jnp.broadcast_to(line[n : n + 1], (32, 256)), 0.0)
-                    w_ref[4 * t + u, pl.ds(tap * 512 + n * 32, 32)] = piece.astype(BF16)
+                    spread = jnp.broadcast_to(line[n : n + 1], (16, 256)).astype(BF16)
+                    w_ref[4 * t + u, pl.ds(tap * 512 + n * 32, 32)] = eye * jnp.concatenate([spread, spread], axis=0)
         return carry
 
     lax.fori_loop(0, 7, body, 0)
 
 
-def fill_rows(tile_of, west, east, xt_ref, row):
-    first = iota((16, 256), 0) == 0
-    last = iota((16, 256), 0) == 15
-    plain = [tile_of(j) for j in range(8)]
-    zero_view, one_view = [None] * 8, [None] * 8
-    for p in range(8):
-        if p < 3:
-            data = plain[p + 5]
-            one_view[p] = data
-            edge = jnp.broadcast_to(west(p), (16, 256))
-            zero_view[p] = jnp.where(first, edge, pltpu.roll(data.astype(F32), 1, 0)).astype(BF16)
-        else:
-            data = plain[p - 3]
-            zero_view[p] = data
-            rolled = pltpu.roll(data.astype(F32), 15, 0)
-            if p < 6:
-                rolled = jnp.where(last, jnp.broadcast_to(east(p - 3), (16, 256)), rolled)
-            one_view[p] = rolled.astype(BF16)
-    for q, view in enumerate((zero_view, one_view)):
-        for t in range(2):
-            for h in range(2):
-                done = swap_blocks([view[4 * h + i][:, 128 * t : 128 * t + 128] for i in range(4)])
-                for u in range(4):
-                    xt_ref[q, 4 * t + u, row, :, 128 * h : 128 * h + 128] = done[u]
-
-
-def block_body(last, kernel_ref, bias_ref, gain_ref, scale_ref, up_ref, down_ref, mask_ref, x_ref, arrived, halo,
-               out_ref, edge_ref, w_ref, xt_ref, conv_ref, stat_ref, rms_ref, side_ref, corner_ref, lines_ref):
+def fill_rows(pad_ref, side_ref, xt_ref):
+    source, target = iota((512, 512), 0), iota((512, 512), 1)
+    moved = (source // 32 % 4) * 128 + (source // 128) * 32 + source % 32
+    mixer = jnp.where(moved == target, 1.0, 0.0).astype(BF16)
+    place = iota((608, 128), 0) % 16
+    first, last, low = place == 0, place == 15, iota((608, 128), 1) < 96
+    for t in range(2):
+        lanes = slice(128 * t, 128 * t + 128)
+        for h in range(2):
+            tiles = [pad_ref[:, (p + 5) % 8, :, lanes].reshape(608, 128) for p in range(4 * h, 4 * h + 4)]
+            mixed = jnp.dot(jnp.concatenate(tiles, axis=1), mixer, preferred_element_type=F32)
+            edges = swap_blocks([side_ref[n, :, lanes] for n in ((0, 1, 2, 3) if h == 0 else (4, 5, 5, 5))])
+            for u in range(4):
+                part = mixed[:, 128 * u : 128 * u + 128]
+                edge = jnp.broadcast_to(edges[u][0:38].reshape(38, 1, 128), (38, 16, 128)).reshape(608, 128)
+                later = jnp.where(last, edge, pltpu.roll(part, 607, 0))
+                if h == 0:
+                    zero_view = jnp.where(low, jnp.where(first, edge, pltpu.roll(part, 1, 0)), part)
+                    one_view = jnp.where(low, part, later)
+                else:
+                    zero_view, one_view = part, later
+                for q, view in enumerate((zero_view, one_view)):
+                    xt_ref[q, 4 * t + u, :, :, 128 * h : 128 * h + 128] = view.astype(BF16).reshape(38, 16, 128)
+
+
+def block_body(last, kernel_ref, bias_ref, gain_ref, scale_ref, up_ref, down_ref, mask_ref, arrived, sides,
+               out_ref, edge_ref, pad_ref, w_ref, xt_ref, conv_ref, stat_ref, rms_ref, side_ref, lines_ref):
     block = 1 if last else 0
     build_weights(block, kernel_ref, w_ref)
     arrived()
-    north_ref, south_ref, west_ref, east_ref, nw_ref, ne_ref, sw_ref, se_ref = halo
-    side_ref[0:3] = west_ref[...].astype(F32)
-    side_ref[3:6] = east_ref[...].astype(F32)
-    for n, ref in enumerate((nw_ref, ne_ref, sw_ref, se_ref)):
-        corner_ref[3 * n : 3 * n + 3] = ref[...].astype(F32)
-
-    def interior(r, carry):
-        fill_rows(lambda j: x_ref[r, j], lambda p: side_ref[p, pl.ds(r, 1)], lambda p: side_ref[3 + p, pl.ds(r, 1)], xt_ref, r + 3)
-        return carry
-
-    lax.fori_loop(0, 32, interior, 0, unroll=2)
-
-    def outer(k, carry):
-        fill_rows(lambda j: north_ref[k, j], lambda p: corner_ref[p, pl.ds(13 + k, 1)], lambda p: corner_ref[3 + p, pl.ds(13 + k, 1)], xt_ref, k)
-        fill_rows(lambda j: south_ref[k, j], lambda p: corner_ref[6 + p, pl.ds(k, 1)], lambda p: corner_ref[9 + p, pl.ds(k, 1)], xt_ref, 35 + k)
-        return carry
-
-    lax.fori_loop(0, 3, outer, 0)
+    west_ref, east_ref, nw_ref, ne_ref, sw_ref, se_ref = sides
+    side_ref[0:3, 3:35] = west_ref[...].astype(F32)
+    side_ref[3:6, 3:35] = east_ref[...].astype(F32)
+    for at, north_ref, south_ref in ((0, nw_ref, sw_ref), (3, ne_ref, se_ref)):
+        side_ref[at : at + 3, 0:3] = north_ref[...].astype(F32)[:, 13:16]
+        side_ref[at : at + 3, 35:38] = south_ref[...].astype(F32)[:, 0:3]
+    side_ref[:, 38:40] = jnp.zeros((6, 2, 256), F32)
+    fill_rows(pad_ref, side_ref, xt_ref)
 
     grouped = []
     lines = jnp.concatenate([bias_ref[block : block + 1]] + [gain_ref[block : block + 1]] * 7, axis=0)
-    scale = scale_ref[block : block + 1]
+    scale = 0.5 * scale_ref[block : block + 1]
     for t in range(2):
         part = lines[:, 128 * t : 128 * t + 128]
         grouped += [jnp.concatenate([v, v], axis=1) for v in swap_blocks([part] * 4)]
@@ -161,11 +150,12 @@
         full = [jnp.concatenate(pair, axis=1) for pair in tiles]
         rows = jnp.concatenate([full[j][16 * k : 16 * k + 16] for k in range(4) for j in range(8)], axis=0)
         wide = jnp.dot(rows, up_ref[block], preferred_element_type=F32)
-        grown = jax.nn.gelu(wide).astype(BF16)
+        wide = wide.astype(BF16)
+        grown = wide + wide * jnp.tanh(wide * (0.7978845608028654 + 0.035677408136300125 * wide * wide))
         small = jnp.dot(grown, down_ref[block], preferred_element_type=F32)
         picks = jnp.concatenate([order * mask_ref[pl.ds(4 * n + k, 1)].astype(F32) for k in range(4)], axis=0).astype(BF16)
         sea = jnp.dot(picks, ones, preferred_element_type=F32)
-        base = x_ref[pl.ds(4 * n, 4)].reshape(512, 256).astype(F32)
+        base = pad_ref[pl.ds(3 + 4 * n, 4)].reshape(512, 256).astype(F32)
         fresh = sea * (base + scale * small)
         fresh16 = fresh.astype(BF16)
         if last:
@@ -178,7 +168,7 @@
                 keep_edges(lines_ref, 4 * n + k, fresh[128 * k : 128 * k + 128], (0, 16, 32, 95, 111, 127))
         return carry
 
-    lax.fori_loop(0, 8, mlp, 0, unroll=2)
+    lax.fori_loop(0, 8, mlp, 0, unroll=4)
     if not last:
         edge_ref[...] = lines_ref[...].astype(BF16)
 
@@ -216,10 +206,12 @@
 
 
 AROUND = [(dr, dc) for dr in (-1, 0, 1) for dc in (-1, 0, 1) if (dr, dc) != (0, 0)]
-HALO = [((3, 8, 16, 256), BF16)] * 2 + [((3, 32, 256), BF16)] * 2 + [((3, 16, 256), BF16)] * 4
+ROWS = [((3, 8, 16, 256), BF16)] * 2
+SIDES = [((3, 32, 256), BF16)] * 2 + [((3, 16, 256), BF16)] * 4
 BLOCK_SCRATCH = [
+    ((38, 8, 16, 256), BF16),
     ((8, 3584, 256), BF16), ((2, 8, 38, 16, 256), BF16), ((8, 512, 256), F32), ((512, 256), F32), ((512, 256), F32),
-    ((6, 32, 256), F32), ((12, 16, 256), F32), ((6, 32, 256), F32)]
+    ((6, 40, 256), F32), ((6, 32, 256), F32)]
 
 
 def greet(devices):
@@ -258,33 +250,37 @@
 def first_kernel(*refs):
     ins, x_ref, edge_ref, norm_ref = refs[:7], refs[7], refs[8], refs[9]
     out_ref, line_ref, rims_ref = refs[10:13]
-    scratch, halo = refs[13:21], refs[21:29]
-    send_sem, recv_sem = refs[29], refs[30]
+    scratch, sides = refs[13:21], refs[21:27]
+    send_sem, recv_sem, local_sem = refs[27:30]
+    pad_ref = scratch[0]
+    own = pltpu.make_async_copy(x_ref, pad_ref.at[pl.ds(3, 32)], local_sem)
+    own.start()
     greet([neighbour(dr, dc) for dr, dc in AROUND])
-    copies = start_halo(x_ref, edge_ref, halo, send_sem, recv_sem)
+    copies = start_halo(x_ref, edge_ref, (pad_ref.at[pl.ds(0, 3)], pad_ref.at[pl.ds(35, 3)]) + tuple(sides), send_sem, recv_sem)
     rims = []
-    for n, (dr, dc) in enumerate(AROUND):
-        slot = (1 - dr) * 3 + 1 - dc
-        slot = slot - 1 if slot > 4 else slot
-        rims.append(send(norm_ref.at[pl.ds(0, 64)], rims_ref.at[slot], send_sem.at[8 + n], recv_sem.at[8 + n], neighbour(dr, dc)))
 
     def arrived():
+        own.wait()
         for copy in copies:
             copy.wait()
-
-    block_body(False, *ins, x_ref, arrived, halo, out_ref, line_ref, *scratch)
+        for n, (dr, dc) in enumerate(AROUND):
+            slot = (1 - dr) * 3 + 1 - dc
+            slot = slot - 1 if slot > 4 else slot
+            rims.append(send(norm_ref.at[pl.ds(0, 64)], rims_ref.at[slot], send_sem.at[8 + n], recv_sem.at[8 + n], neighbour(dr, dc)))
+
+    block_body(False, *ins, arrived, sides, out_ref, line_ref, *scratch)
     for copy in rims:
         copy.wait()
 
 
 def ocean_first(*args):
-    scratch = [pltpu.VMEM(*item) for item in BLOCK_SCRATCH + HALO] + [pltpu.SemaphoreType.DMA((16,))] * 2
+    scratch = [pltpu.VMEM(*item) for item in BLOCK_SCRATCH + SIDES] + [pltpu.SemaphoreType.DMA((16,))] * 2 + [pltpu.SemaphoreType.DMA]
     return pl.pallas_call(
         first_kernel,
         out_shape=(
             jax.ShapeDtypeStruct((32, 8, 16, 256), BF16), jax.ShapeDtypeStruct((6, 32, 256), BF16),
             jax.ShapeDtypeStruct((8, 64, 512), BF16)),
-        in_specs=[vmem()] * len(args),
+        in_specs=[vmem()] * 7 + [anywhere(), vmem(), vmem()],
         out_specs=(vmem(), vmem(), anywhere()),
         scratch_shapes=scratch,
         compiler_params=pltpu.CompilerParams(vmem_limit_bytes=60 << 20, collective_id=1, has_side_effects=True),
@@ -293,17 +289,30 @@
 
 
 def last_kernel(*refs):
-    ins, x_ref, halo, out_ref, scratch = refs[:7], refs[7], refs[8:16], refs[16], refs[17:]
-    block_body(True, *ins, x_ref, lambda: None, halo, out_ref, None, *scratch)
+    ins, x_ref, north_ref, south_ref, sides = refs[:7], refs[7], refs[8], refs[9], refs[10:16]
+    out_ref, scratch, sems = refs[16], refs[17:25], refs[25]
+    pad_ref = scratch[0]
+    copies = [
+        pltpu.make_async_copy(x_ref, pad_ref.at[pl.ds(3, 32)], sems.at[0]),
+        pltpu.make_async_copy(north_ref, pad_ref.at[pl.ds(0, 3)], sems.at[1]),
+        pltpu.make_async_copy(south_ref, pad_ref.at[pl.ds(35, 3)], sems.at[2])]
+    for copy in copies:
+        copy.start()
+
+    def arrived():
+        for copy in copies:
+            copy.wait()
+
+    block_body(True, *ins, arrived, sides, out_ref, None, *scratch)
 
 
 def ocean_last(*args):
     return pl.pallas_call(
         last_kernel,
         out_shape=jax.ShapeDtypeStruct((32, 128, 256), BF16),
-        in_specs=[vmem()] * len(args),
+        in_specs=[vmem()] * 7 + [anywhere()] * 3 + [vmem()] * 6,
         out_specs=vmem(),
-        scratch_shapes=[pltpu.VMEM(*item) for item in BLOCK_SCRATCH],
+        scratch_shapes=[pltpu.VMEM(*item) for item in BLOCK_SCRATCH] + [pltpu.SemaphoreType.DMA((3,))],
         compiler_params=pltpu.CompilerParams(vmem_limit_bytes=60 << 20),
         name="ocean_last",
     )(*args)
@@ -372,12 +381,12 @@
         keep_edges(lines_ref, r, fresh, (0, 1, 2, 125, 126, 127))
         return carry
 
-    lax.fori_loop(0, 16, row, 0, unroll=2)
+    lax.fori_loop(0, 16, row, 0, unroll=8)
     for step in range(1, 8):
         field_copies[step - 1].wait()
         block = field_tab.at[side * 8 + lax.rem(deep + 8 - step, 8)]
         pass_copies.append(send(block, block, pass_send.at[step], pass_recv.at[step], partner))
-    lax.fori_loop(16, 32, row, 0, unroll=2)
+    lax.fori_loop(16, 32, row, 0, unroll=8)
     edge_ref[...] = lines_ref[...].astype(BF16)
     for copy in pass_copies:
         copy.wait()
@@ -494,7 +503,7 @@
     return pl.pallas_call(
         atmosphere_kernel,
         out_shape=(jax.ShapeDtypeStruct((128, 512), BF16), jax.ShapeDtypeStruct((6, 128, 512), BF16))
-        + tuple(jax.ShapeDtypeStruct(*item) for item in HALO),
+        + tuple(jax.ShapeDtypeStruct(*item) for item in ROWS + SIDES),
         in_specs=[vmem()] * (len(args) - 2) + [anywhere()] * 2,
         out_specs=(vmem(), vmem()) + (anywhere(),) * 8,
         scratch_shapes=[pltpu.SemaphoreType.DMA((8,))] * 2,

time: 121 us -> 103 us (0.85)
  Pallas kernels: 119 us -> 99.9 us
    pallas_call x1, Pallas kernels: 39.4 us -> 32.1 us  [ocean_first(): pl.pallas_call(first_kernel, out_shape=(jax.ShapeDtypeStruct((32, 8, 16,...]
    pallas_call x1, Pallas kernels: 30.1 us -> 24.6 us  [ocean_last(): pl.pallas_call(last_kernel, out_shape=jax.ShapeDtypeStruct((32, 128, 256)...]
    pallas_call x1, Pallas kernels: 31.5 us -> 26.8 us  [front(): pl.pallas_call(front_kernel, out_shape=(jax.ShapeDtypeStruct((32, 8, 16,...]
    pallas_call x1, Pallas kernels: 17.9 us -> 16.5 us  [atmosphere(): pl.pallas_call(atmosphere_kernel, out_shape=(jax.ShapeDtypeStruct((128, 5...]
where the time goes in v2:
time: 103 us; the launch traced here: 102 us
  Pallas kernels  99.9 us (97%)
  local copies, waits for them, and re-layouts  1.55 us (2%)
    pallas_call x1, Pallas kernels, ocean_first(): pl.pallas_call(first_kernel, out_shape=(jax.ShapeDtypeStruct((32, 8, 16,...  32.1 us
    pallas_call x1, Pallas kernels, front(): pl.pallas_call(front_kernel, out_shape=(jax.ShapeDtypeStruct((32, 8, 16,...  26.8 us
    pallas_call x1, Pallas kernels, ocean_last(): pl.pallas_call(last_kernel, out_shape=jax.ShapeDtypeStruct((32, 128, 256)...  24.6 us
    pallas_call x1, Pallas kernels, atmosphere(): pl.pallas_call(atmosphere_kernel, out_shape=(jax.ShapeDtypeStruct((128, 5...  16.5 us

profile of v2, /device:TPU:1, one launch (start us, length us, event | category | flops | bytes accessed | tf_op | source)
XLA Modules:
  0.0 102.2 jit_solution(5425037316643060916)
XLA Ops:
  0.6 26.8 %front.1 = (bf16[32,8,16,256]{3,2,1,0:T(8,128)(2,1)}, bf16[6,32,256]{2,1,0:T(8,128)(2,1)}, f32[128,512]{1,0:T(8,128)}, bf16[128,512]{1,0:T(8,128)(2,1)}) custom-call(f32[4,512]{1,0:T(4,128)} %bitcast.18, f32[128,128]{1,0:T(8,128)} %bitcast.16, s32[4,32,128]{2,1,0:T(8,128)} %cols_ref.1, f32[4,32,128]{2,1,0:T(8,128)} %fluxw_ref.1, ...), custom_call_target="tpu_custom_call" | custom-call | tf_op jit(solution)/shard_map/front/pallas_call | solution.py:420
  27.4 32.1 %ocean_first.1 = (bf16[32,8,16,256]{3,2,1,0:T(8,128)(2,1)}, bf16[6,32,256]{2,1,0:T(8,128)(2,1)}, bf16[8,64,512]{2,1,0:T(8,128)(2,1)}) custom-call(f32[49,2,256]{2,1,0:T(2,128)} %bitcast.14, f32[2,256]{1,0:T(2,128)} %refs_1_.3, f32[2,256]{1,0:T(2,128)} %refs_2_.3, f32[2,256]{1,0:T(2,128)} %refs_3_.3, bf16[2,256,1024]{2,1,0:T(8,128)(2,1)} %refs_4_.3, ...), custom_call_target="tpu_custom_call" | custom-call | tf_op jit(solution)/shard_map/ocean_first/pallas_call | solution.py:278
  59.6 16.5 %atmosphere.1 = (bf16[128,512]{1,0:T(8,128)(2,1)}, bf16[6,128,512]{2,1,0:T(8,128)(2,1)}, bf16[3,8,16,256]{3,2,1,0:T(8,128)(2,1)}, bf16[3,8,16,256]{3,2,1,0:T(8,1...) custom-call(bf16[128,512]{1,0:T(8,128)(2,1)} %get-tuple-element.20.r, ...), custom_call_target="tpu_custom_call" | custom-call | tf_op jit(solution)/shard_map/atmosphere/pallas_call | solution.py:503
  76.0 0.0 copy-start.1
  76.0 0.0 copy-start
  76.0 24.6 %ocean_last.1 = bf16[32,128,256]{2,1,0:T(8,128)(2,1)} custom-call(f32[49,2,256]{2,1,0:T(2,128)} %bitcast.15, f32[2,256]{1,0:T(2,128)} %refs_1_.3, f32[2,256]{1,0:T(2,128)} %refs_2_.3, f32[2,256]{1,0:T(2,128)} %refs_3_.3, bf16[2,256,1024]{2,1,0:T(8,128)(2,1)} %refs_4_.3, bf16[2,1024,256]{2,1,0:T(8,128)(2,1)} %refs_5_.3, s32[32,128]{1,0:T(8,128)} %refs_6_.3, ...), custom_call_target="tpu_custom_call" | custom-call | tf_op jit(solution)/shard_map/ocean_last/pallas_call | solution.py:310
  100.6 0.0 copy-done.1
  100.6 0.7 copy.38
  101.3 0.0 copy-done
  101.3 0.9 copy.39
Async XLA Ops:
  76.0 24.6 %copy-start.1 = (bf16[128,512]{1,0:T(8,128)(2,1)S(1)}, bf16[128,512]{1,0:T(8,128)(2,1)}, u32[]{:S(2)}) copy-start(bf16[128,512]{1,0:T(8,128)(2,1)} %get-tuple-element.40) | copy-start | bytes 393220
  76.0 25.3 %copy-start = (bf16[6,128,512]{2,1,0:T(8,128)(2,1)S(1)}, bf16[6,128,512]{2,1,0:T(8,128)(2,1)}, u32[]{:S(2)}) copy-start(bf16[6,128,512]{2,1,0:T(8,128)(2,1)} %get-tuple-element.28) | copy-start | bytes 2359300

commit v3 on v2

--- a/solution.py
+++ b/solution.py
@@ -81,7 +81,7 @@
                     xt_ref[q, 4 * t + u, :, :, 128 * h : 128 * h + 128] = view.astype(BF16).reshape(38, 16, 128)
 
 
-def block_body(last, kernel_ref, bias_ref, gain_ref, scale_ref, up_ref, down_ref, mask_ref, arrived, sides,
+def block_body(last, kernel_ref, bias_ref, gain_ref, scale_ref, up_ref, down_ref, mask_ref, arrived, landed, sides,
                out_ref, edge_ref, pad_ref, w_ref, xt_ref, conv_ref, stat_ref, rms_ref, side_ref, lines_ref):
     block = 1 if last else 0
     build_weights(block, kernel_ref, w_ref)
@@ -149,10 +149,10 @@
                     tiles[4 * h + i][t] = done[i]
         full = [jnp.concatenate(pair, axis=1) for pair in tiles]
         rows = jnp.concatenate([full[j][16 * k : 16 * k + 16] for k in range(4) for j in range(8)], axis=0)
-        wide = jnp.dot(rows, up_ref[block], preferred_element_type=F32)
+        wide = jnp.dot(rows, up_ref[...], preferred_element_type=F32)
         wide = wide.astype(BF16)
         grown = wide + wide * jnp.tanh(wide * (0.7978845608028654 + 0.035677408136300125 * wide * wide))
-        small = jnp.dot(grown, down_ref[block], preferred_element_type=F32)
+        small = jnp.dot(grown, down_ref[...], preferred_element_type=F32)
         picks = jnp.concatenate([order * mask_ref[pl.ds(4 * n + k, 1)].astype(F32) for k in range(4)], axis=0).astype(BF16)
         sea = jnp.dot(picks, ones, preferred_element_type=F32)
         base = pad_ref[pl.ds(3 + 4 * n, 4)].reshape(512, 256).astype(F32)
@@ -168,6 +168,7 @@
                 keep_edges(lines_ref, 4 * n + k, fresh[128 * k : 128 * k + 128], (0, 16, 32, 95, 111, 127))
         return carry
 
+    landed()
     lax.fori_loop(0, 8, mlp, 0, unroll=4)
     if not last:
         edge_ref[...] = lines_ref[...].astype(BF16)
@@ -214,11 +215,26 @@
     ((6, 40, 256), F32), ((6, 32, 256), F32)]
 
 
+WEIGHT_SCRATCH = [pltpu.VMEM((256, 1024), BF16), pltpu.VMEM((1024, 256), BF16), pltpu.SemaphoreType.DMA((2,))]
+
+
 def greet(devices):
     barrier = pltpu.get_barrier_semaphore()
     for device in devices:
         pl.semaphore_signal(barrier, inc=1, device_id=device, device_id_type=pl.DeviceIdType.MESH)
     pl.semaphore_wait(barrier, len(devices))
+
+
+def fetch(sources, targets, sems):
+    copies = [pltpu.make_async_copy(source, target, sems.at[n]) for n, (source, target) in enumerate(zip(sources, targets))]
+    for copy in copies:
+        copy.start()
+
+    def landed():
+        for copy in copies:
+            copy.wait()
+
+    return landed
 
 
 def neighbour(dr, dc):
@@ -251,12 +267,13 @@
     ins, x_ref, edge_ref, norm_ref = refs[:7], refs[7], refs[8], refs[9]
     out_ref, line_ref, rims_ref = refs[10:13]
     scratch, sides = refs[13:21], refs[21:27]
-    send_sem, recv_sem, local_sem = refs[27:30]
+    send_sem, recv_sem, local_sem, up_buf, down_buf, weight_sem = refs[27:33]
     pad_ref = scratch[0]
     own = pltpu.make_async_copy(x_ref, pad_ref.at[pl.ds(3, 32)], local_sem)
     own.start()
     greet([neighbour(dr, dc) for dr, dc in AROUND])
     copies = start_halo(x_ref, edge_ref, (pad_ref.at[pl.ds(0, 3)], pad_ref.at[pl.ds(35, 3)]) + tuple(sides), send_sem, recv_sem)
+    landed = fetch((ins[4].at[0], ins[5].at[0]), (up_buf, down_buf), weight_sem)
     rims = []
 
     def arrived():
@@ -268,19 +285,19 @@
             slot = slot - 1 if slot > 4 else slot
             rims.append(send(norm_ref.at[pl.ds(0, 64)], rims_ref.at[slot], send_sem.at[8 + n], recv_sem.at[8 + n], neighbour(dr, dc)))
 
-    block_body(False, *ins, arrived, sides, out_ref, line_ref, *scratch)
+    block_body(False, *ins[:4], up_buf, down_buf, ins[6], arrived, landed, sides, out_ref, line_ref, *scratch)
     for copy in rims:
         copy.wait()
 
 
 def ocean_first(*args):
-    scratch = [pltpu.VMEM(*item) for item in BLOCK_SCRATCH + SIDES] + [pltpu.SemaphoreType.DMA((16,))] * 2 + [pltpu.SemaphoreType.DMA]
+    scratch = [pltpu.VMEM(*item) for item in BLOCK_SCRATCH + SIDES] + [pltpu.SemaphoreType.DMA((16,))] * 2 + [pltpu.SemaphoreType.DMA] + WEIGHT_SCRATCH
     return pl.pallas_call(
         first_kernel,
         out_shape=(
             jax.ShapeDtypeStruct((32, 8, 16, 256), BF16), jax.ShapeDtypeStruct((6, 32, 256), BF16),
             jax.ShapeDtypeStruct((8, 64, 512), BF16)),
-        in_specs=[vmem()] * 7 + [anywhere(), vmem(), vmem()],
+        in_specs=[vmem()] * 4 + [anywhere()] * 2 + [vmem(), anywhere(), vmem(), vmem()],
         out_specs=(vmem(), vmem(), anywhere()),
         scratch_shapes=scratch,
         compiler_params=pltpu.CompilerParams(vmem_limit_bytes=60 << 20, collective_id=1, has_side_effects=True),
@@ -291,6 +308,7 @@
 def last_kernel(*refs):
     ins, x_ref, north_ref, south_ref, sides = refs[:7], refs[7], refs[8], refs[9], refs[10:16]
     out_ref, scratch, sems = refs[16], refs[17:25], refs[25]
+    up_buf, down_buf, weight_sem = refs[26:29]
     pad_ref = scratch[0]
     copies = [
         pltpu.make_async_copy(x_ref, pad_ref.at[pl.ds(3, 32)], sems.at[0]),
@@ -303,24 +321,26 @@
         for copy in copies:
             copy.wait()
 
-    block_body(True, *ins, arrived, sides, out_ref, None, *scratch)
+    landed = fetch((ins[4].at[1], ins[5].at[1]), (up_buf, down_buf), weight_sem)
+    block_body(True, *ins[:4], up_buf, down_buf, ins[6], arrived, landed, sides, out_ref, None, *scratch)
 
 
 def ocean_last(*args):
     return pl.pallas_call(
         last_kernel,
         out_shape=jax.ShapeDtypeStruct((32, 128, 256), BF16),
-        in_specs=[vmem()] * 7 + [anywhere()] * 3 + [vmem()] * 6,
+        in_specs=[vmem()] * 4 + [anywhere()] * 2 + [vmem()] + [anywhere()] * 3 + [vmem()] * 6,
         out_specs=vmem(),
-        scratch_shapes=[pltpu.VMEM(*item) for item in BLOCK_SCRATCH] + [pltpu.SemaphoreType.DMA((3,))],
+        scratch_shapes=[pltpu.VMEM(*item) for item in BLOCK_SCRATCH] + [pltpu.SemaphoreType.DMA((3,))] + WEIGHT_SCRATCH,
         compiler_params=pltpu.CompilerParams(vmem_limit_bytes=60 << 20),
         name="ocean_last",
     )(*args)
 
 
-def front_kernel(wflux_ref, fields_ref, cols_ref, fluxw_ref, ocean_ref, mask_ref, wfin_ref, scols_ref, sw_ref, state_ref, wsurf_ref,
+def front_kernel(wflux_ref, fields_ref, cols_ref, fluxw_ref, state_hbm, mask_ref, wfin_ref, scols_ref, sw_ref, state_ref, wsurf_ref,
                  gain_ref, x_ref, edge_ref, atm_ref, norm_ref, flux_own, field_own, flux_tab, field_tab, lines_ref,
-                 flux_send, flux_recv, field_send, field_recv, pass_send, pass_recv):
+                 flux_send, flux_recv, field_send, field_recv, pass_send, pass_recv, ocean_ref, ocean_sem):
+    landed = fetch((state_hbm,), (ocean_ref,), ocean_sem)
     me = lax.axis_index("lon")
     side, deep = me // 8, lax.rem(me, 8)
     partner = {"lon": lax.rem(me + 8, 16)}
@@ -342,6 +362,7 @@
     pass_copies = [send(field_own, field_tab.at[me], pass_send.at[0], pass_recv.at[0], partner)]
     for copy in small_copies:
         copy.wait()
+    landed()
 
     pairs = []
     for p in range(8):
@@ -425,11 +446,12 @@
             jax.ShapeDtypeStruct((128, 512), F32),
             jax.ShapeDtypeStruct((128, 512), BF16),
         ),
-        in_specs=[vmem()] * len(args),
+        in_specs=[vmem()] * 4 + [anywhere()] + [vmem()] * (len(args) - 5),
         out_specs=tuple([vmem()] * 4),
         scratch_shapes=[
             pltpu.VMEM((16, 128), BF16), pltpu.VMEM((128, 128), BF16), pltpu.VMEM((16, 16, 128), BF16), pltpu.VMEM((16, 128, 128), BF16),
-            pltpu.VMEM((6, 32, 256), F32)] + [pltpu.SemaphoreType.DMA((16,))] * 2 + [pltpu.SemaphoreType.DMA((8,))] * 4,
+            pltpu.VMEM((6, 32, 256), F32)] + [pltpu.SemaphoreType.DMA((16,))] * 2 + [pltpu.SemaphoreType.DMA((8,))] * 4
+        + [pltpu.VMEM((32, 128, 256), BF16), pltpu.SemaphoreType.DMA((1,))],
         compiler_params=pltpu.CompilerParams(vmem_limit_bytes=60 << 20, collective_id=0, has_side_effects=True),
         name="front",
     )(*args)
@@ -439,10 +461,14 @@
     return values * jax.nn.sigmoid(values)
 
 
-def atmosphere_kernel(norm_ref, rims_ref, atm_ref, edges_ref, near_ref, degree_ref, wq_ref, wk_ref, wv_ref, wo_ref, win_ref, wsrc_ref,
-                      wdst_ref, wout_ref, wbias_ref, gain_ref, up_ref, down_ref, x_ref, line_ref, out_ref, edge_out_ref, *rest):
+def atmosphere_kernel(norm_ref, rims_ref, atm_ref, edges_hbm, near_ref, degree_ref, wq_hbm, wk_hbm, wv_hbm, wo_hbm, win_hbm, wsrc_hbm,
+                      wdst_hbm, wout_hbm, wbias_ref, gain_ref, up_hbm, down_hbm, x_ref, line_ref, out_ref, edge_out_ref, *rest):
     greet([neighbour(dr, dc) for dr, dc in AROUND])
     copies = start_halo(x_ref, line_ref, rest[:8], rest[8], rest[9])
+    early = (wk_hbm, wv_hbm, wdst_hbm, wq_hbm, wsrc_hbm, edges_hbm, win_hbm, wout_hbm)
+    ready = fetch(early, rest[10:18], rest[21])
+    ready_late = fetch((wo_hbm, up_hbm, down_hbm), rest[18:21], rest[22])
+    wk_ref, wv_ref, wdst_ref, wq_ref, wsrc_ref, edges_ref, win_ref, wout_ref, wo_ref, up_ref, down_ref = rest[10:21]
     band = lax.axis_index("comp") * 8 + lax.axis_index("lat")
     col = lax.axis_index("lon")
     ids = near_ref[...]
@@ -458,6 +484,7 @@
     lane = iota((128, 640), 1).astype(F32)
     hots = [jnp.where(lane == info[:, k : k + 1], 1.0, 0.0).astype(BF16) for k in range(6)]
     near = jnp.dot(jnp.concatenate(hots, axis=0), table, preferred_element_type=F32).astype(BF16)
+    ready()
     keys = jnp.dot(near, wk_ref[...], preferred_element_type=F32).astype(BF16)
     values = jnp.dot(near, wv_ref[...], preferred_element_type=F32).astype(BF16)
     far = jnp.dot(near, wdst_ref[...], preferred_element_type=F32).astype(BF16)
@@ -491,6 +518,7 @@
         spread = jnp.dot(weight, head.astype(BF16), preferred_element_type=F32)
         term = spread * values[128 * k : 128 * k + 128].astype(F32)
         attended = term if attended is None else attended + term
+    ready_late()
     middle = atm_ref[...] + jnp.dot(attended.astype(BF16), wo_ref[...], preferred_element_type=F32)
     normed2 = unit_norm(middle, gain_ref[...], 1e-5).astype(BF16)
     expanded = silu(jnp.dot(normed2, up_ref[...], preferred_element_type=F32)).astype(BF16)
@@ -504,9 +532,11 @@
         atmosphere_kernel,
         out_shape=(jax.ShapeDtypeStruct((128, 512), BF16), jax.ShapeDtypeStruct((6, 128, 512), BF16))
         + tuple(jax.ShapeDtypeStruct(*item) for item in ROWS + SIDES),
-        in_specs=[vmem()] * (len(args) - 2) + [anywhere()] * 2,
+        in_specs=[vmem()] * 3 + [anywhere()] + [vmem()] * 2 + [anywhere()] * 8 + [vmem()] * 2 + [anywhere()] * 4,
         out_specs=(vmem(), vmem()) + (anywhere(),) * 8,
-        scratch_shapes=[pltpu.SemaphoreType.DMA((8,))] * 2,
+        scratch_shapes=[pltpu.SemaphoreType.DMA((8,))] * 2 + [pltpu.VMEM((512, 512), BF16)] * 5 + [pltpu.VMEM((6, 128, 512), BF16)]
+        + [pltpu.VMEM((512, 512), BF16)] * 3 + [pltpu.VMEM((512, 2048), BF16), pltpu.VMEM((2048, 512), BF16)]
+        + [pltpu.SemaphoreType.DMA((8,)), pltpu.SemaphoreType.DMA((3,))],
         compiler_params=pltpu.CompilerParams(vmem_limit_bytes=60 << 20, collective_id=2, has_side_effects=True),
         name="atmosphere",
     )(*args)

time: 103 us -> 100 us (0.971)
  Pallas kernels: 99.9 us -> 97.7 us
where the time goes in v3:
time: 100 us; the launch traced here: 99.9 us
  Pallas kernels  97.7 us (98%)
  local copies, waits for them, and re-layouts  1.55 us (2%)
    pallas_call x1, Pallas kernels, ocean_first(): pl.pallas_call(first_kernel, out_shape=(jax.ShapeDtypeStruct((32, 8, 16,...  31.6 us
    pallas_call x1, Pallas kernels, front(): pl.pallas_call(front_kernel, out_shape=(jax.ShapeDtypeStruct((32, 8, 16,...  26.1 us
    pallas_call x1, Pallas kernels, ocean_last(): pl.pallas_call(last_kernel, out_shape=jax.ShapeDtypeStruct((32, 128, 256)...  24 us
    pallas_call x1, Pallas kernels, atmosphere(): pl.pallas_call(atmosphere_kernel, out_shape=(jax.ShapeDtypeStruct((128, 5...  16.1 us

profile of v3, /device:TPU:1, one launch (start us, length us, event | category | flops | bytes accessed | tf_op | source)
XLA Modules:
  0.0 99.9 jit_solution(7613809228686077109)
XLA Ops:
  0.6 26.1 %front.1 = (bf16[32,8,16,256]{3,2,1,0:T(8,128)(2,1)}, bf16[6,32,256]{2,1,0:T(8,128)(2,1)}, f32[128,512]{1,0:T(8,128)}, bf16[128,512]{1,0:T(8,128)(2,1)}) custom-call(f32[4,512]{1,0:T(4,128)} %bitcast.18, f32[128,128]{1,0:T(8,128)} %bitcast.16, s32[4,32,128]{2,1,0:T(8,128)} %cols_ref.1, f32[4,32,128]{2,1,0:T(8,128)} %fluxw_ref.1, ...), custom_call_target="tpu_custom_call" | custom-call | tf_op jit(solution)/shard_map/front/pallas_call | solution.py:441
  26.7 31.6 %ocean_first.1 = (bf16[32,8,16,256]{3,2,1,0:T(8,128)(2,1)}, bf16[6,32,256]{2,1,0:T(8,128)(2,1)}, bf16[8,64,512]{2,1,0:T(8,128)(2,1)}) custom-call(f32[49,2,256]{2,1,0:T(2,128)} %bitcast.14, f32[2,256]{1,0:T(2,128)} %refs_1_.3, f32[2,256]{1,0:T(2,128)} %refs_2_.3, f32[2,256]{1,0:T(2,128)} %refs_3_.3, bf16[2,256,1024]{2,1,0:T(8,128)(2,1)} %refs_4_.3, ...), custom_call_target="tpu_custom_call" | custom-call | tf_op jit(solution)/shard_map/ocean_first/pallas_call | solution.py:295
  58.3 16.1 %atmosphere.1 = (bf16[128,512]{1,0:T(8,128)(2,1)}, bf16[6,128,512]{2,1,0:T(8,128)(2,1)}, bf16[3,8,16,256]{3,2,1,0:T(8,128)(2,1)}, bf16[3,8,16,256]{3,2,1,0:T(8,1...) custom-call(bf16[128,512]{1,0:T(8,128)(2,1)} %get-tuple-element.20.r, ...), custom_call_target="tpu_custom_call" | custom-call | tf_op jit(solution)/shard_map/atmosphere/pallas_call | solution.py:531
  74.4 0.0 copy-start.1
  74.4 0.0 copy-start
  74.4 24.0 %ocean_last.1 = bf16[32,128,256]{2,1,0:T(8,128)(2,1)} custom-call(f32[49,2,256]{2,1,0:T(2,128)} %bitcast.15, f32[2,256]{1,0:T(2,128)} %refs_1_.3, f32[2,256]{1,0:T(2,128)} %refs_2_.3, f32[2,256]{1,0:T(2,128)} %refs_3_.3, bf16[2,256,1024]{2,1,0:T(8,128)(2,1)} %refs_4_.3, bf16[2,1024,256]{2,1,0:T(8,128)(2,1)} %refs_5_.3, s32[32,128]{1,0:T(8,128)} %refs_6_.3, ...), custom_call_target="tpu_custom_call" | custom-call | tf_op jit(solution)/shard_map/ocean_last/pallas_call | solution.py:329
  98.4 0.0 copy-done.1
  98.4 0.7 copy.38
  99.0 0.0 copy-done
  99.0 0.9 copy.39
Async XLA Ops:
  74.4 24.0 %copy-start.1 = (bf16[128,512]{1,0:T(8,128)(2,1)S(1)}, bf16[128,512]{1,0:T(8,128)(2,1)}, u32[]{:S(2)}) copy-start(bf16[128,512]{1,0:T(8,128)(2,1)} %get-tuple-element.40) | copy-start | bytes 393220
  74.4 24.7 %copy-start = (bf16[6,128,512]{2,1,0:T(8,128)(2,1)S(1)}, bf16[6,128,512]{2,1,0:T(8,128)(2,1)}, u32[]{:S(2)}) copy-start(bf16[6,128,512]{2,1,0:T(8,128)(2,1)} %get-tuple-element.28) | copy-start | bytes 2359300
